TPU v7x, 32 devices: a whole 2x2x4 slice. The times are simulated.
32 devices in a mesh: seq: 2 (over x), fsdp: 16 (over z, y, core).
Axes of the slice: x: 2, y: 2, z: 4, core: 2. Of those that a mesh axis runs over, the one named last changes fastest.
Arguments:
- tokens: bfloat16 [4096, 1024], P(('fsdp', 'seq')), may hold values from -6 to 6
- cotangent: bfloat16 [4096, 1024], P(('fsdp', 'seq')), may hold values from -6 to 6
- documents: int32 [16, 256], P('fsdp'), may hold values from 0 to 3, never falling along the last dimension, each value on 1 to 128 neighbouring positions
- in_weight: bfloat16 [1024, 4384], P('fsdp'), may hold values from -0.1875 to 0.1875
- kernel_taps: float32 [4, 2304], replicated, may hold values from -3 to 3
- kernel_bias: float32 [2304], replicated, may hold values from -0.5 to 0.5
- step_bias: float32 [32], replicated, may hold values from -6 to -2
- decay_log: float32 [32], replicated, may hold values from 0 to 2.77
- skip_gain: float32 [32], replicated, may hold values from 0.5 to 1.5
- pre_gain: float32 [1024], replicated, may hold values from 0.5 to 1.5
- norm_gain: float32 [2048], replicated, may hold values from 0.5 to 1.5
- out_weight: bfloat16 [2048, 1024], P('fsdp'), may hold values from -0.125 to 0.125
Outputs:
- block_output: bfloat16 [4096, 1024], P(('fsdp', 'seq'))
- tokens_grad: float32 [4096, 1024], P(('fsdp', 'seq'))
- in_weight_grad: float32 [1024, 4384], P('fsdp')
- kernel_taps_grad: float32 [4, 2304], replicated
- kernel_bias_grad: float32 [2304], replicated
- step_bias_grad: float32 [32], replicated
- decay_log_grad: float32 [32], replicated
- skip_gain_grad: float32 [32], replicated
- pre_gain_grad: float32 [1024], replicated
- norm_gain_grad: float32 [2048], replicated
- out_weight_grad: float32 [2048, 1024], P('fsdp')
Inputs may be any that keep to these rules, and one draw needn't show every extreme that they name: `documents`: in every sequence the ids start at 0 and never fall; each id marks one document of consecutive tokens, and every id of 0 to 3 occurs.
All inputs are finite; a program needn't handle non-finite values.
Results may differ from a plain program's by a relative error of at most 0.011.
Values may be sent and summed in bfloat16 or wider, within the bound.
A program may use at most 128 MiB of HBM per device.

v0:
```python
import functools
import math

import jax
import jax.numpy as jnp
from jax import lax
from jax.experimental import pallas as pl
from jax.experimental.pallas import tpu as pltpu
from jax.sharding import PartitionSpec as P

HEAD_DIM = 64
STATE = 128
CONV = 4
SPAN = 256

norm_epsilon = 1e-05
bf16 = jnp.bfloat16
f32 = jnp.float32
contract_rows = (((1,), (1,)), ((), ()))
contract_tokens = (((0,), (0,)), ((), ()))


def dot(left, right, dims=(((1,), (0,)), ((), ()))):
    return lax.dot_general(left, right, dims, preferred_element_type=f32)


def pre_norm(values, gain):
    scale = lax.rsqrt(jnp.mean(values * values, axis=-1, keepdims=True) + norm_epsilon)
    return values * scale * gain


def product(spec, left, right):
    return jnp.einsum(spec, left.astype(bf16), right.astype(bf16), preferred_element_type=f32)


def mixer(segment, conv_in, step_raw, taps, tap_bias, bias_steps, log_rates, skips):
    length, channels = conv_in.shape
    heads = step_raw.shape[1]
    width = heads * HEAD_DIM
    summed = tap_bias + conv_in * taps[CONV - 1]
    for offset in range(1, CONV):
        shifted = jnp.concatenate(
            [jnp.zeros((offset, channels), f32), conv_in[: length - offset]], axis=0
        )
        matched = jnp.concatenate(
            [
                jnp.zeros((offset,), f32),
                (segment[offset:] == segment[: length - offset]).astype(f32),
            ]
        )
        summed = summed + taps[CONV - 1 - offset] * shifted * matched[:, None]
    active = jax.nn.silu(summed)
    values = active[:, :width].reshape(length, heads, HEAD_DIM).transpose(1, 0, 2)
    input_matrix = active[:, width : width + STATE]
    output_matrix = active[:, width + STATE :]
    steps_taken = jax.nn.softplus(step_raw + bias_steps)
    log_decay = (steps_taken * -jnp.exp(log_rates)).T
    scaled = values * steps_taken.T[:, :, None]
    span = min(SPAN, length)
    blocks = length // span
    places = jnp.arange(span)
    state = None
    outputs = []
    for block in range(blocks):
        at = slice(block * span, (block + 1) * span)
        seg = segment[at]
        cumul = jnp.cumsum(log_decay[:, at], axis=1)
        causal = (places[:, None] >= places[None, :]) & (seg[:, None] == seg[None, :])
        log_gap = cumul[:, :, None] - cumul[:, None, :]
        decay = jnp.where(causal[None], jnp.exp(jnp.where(causal[None], log_gap, 0.0)), 0.0)
        scores = product("in,jn->ij", output_matrix[at], input_matrix[at])
        inside = product("hij,hjp->hip", decay * scores[None], scaled[:, at])
        if state is not None:
            previous = segment[block * span - 1]
            entering = jnp.exp(cumul) * (seg == previous).astype(f32)[None]
            inside = inside + product("in,hnp->hip", output_matrix[at], state) * entering[:, :, None]
        if block + 1 < blocks:
            final = cumul[:, -1]
            leaving = jnp.exp(final[:, None] - cumul) * (seg == seg[-1]).astype(f32)[None]
            fresh = product("jn,hjp->hnp", input_matrix[at], scaled[:, at] * leaving[:, :, None])
            if state is None:
                state = fresh
            else:
                keeping = jnp.exp(final) * (seg[-1] == previous).astype(f32)
                state = keeping[:, None, None] * state + fresh
        outputs.append(inside)
    whole = outputs[0] if blocks == 1 else jnp.concatenate(outputs, axis=1)
    result = whole + values * skips[:, None, None]
    return result.transpose(1, 0, 2).reshape(length, width)

MESH = pl.DeviceIdType.MESH
VMEM_LIMIT = 60 * 1024 * 1024


def factors(shards):
    rest = shards // 2
    mid = 1 << (int(math.log2(rest)) // 2)
    return rest // mid, mid


def position(top, mid):
    me = lax.axis_index("fsdp")
    return me, me // (2 * mid), lax.rem(me // 2, mid), lax.rem(me, 2)


def slot_of(t, m, core, mid):
    return (t * mid + m) * 2 + core


def greet(groups, top, mid):
    me, t, m, core = position(top, mid)
    group = lax.axis_index("seq")
    peers = [{"fsdp": slot_of(lax.rem(t + d, top), m, core, mid)} for d in range(1, top)]
    peers += [{"fsdp": slot_of(t, lax.rem(m + e, mid), core, mid)} for e in range(1, mid)]
    peers += [{"fsdp": slot_of(t, m, 1 - core, mid)}]
    peers += [{"seq": lax.rem(group + k, groups)} for k in range(1, groups)]
    barrier = pltpu.get_barrier_semaphore()
    for peer in peers:
        pl.semaphore_signal(barrier, inc=1, device_id=peer, device_id_type=MESH)
    pl.semaphore_wait(barrier, len(peers))


def remote(source, target, send, receive, device):
    copy = pltpu.make_async_remote_copy(
        src_ref=source,
        dst_ref=target,
        send_sem=send,
        recv_sem=receive,
        device_id=device,
        device_id_type=MESH,
    )
    copy.start()
    return copy


def gather_kernel(groups, top, mid, count, *refs):
    rows, shards = refs[0], refs[1 : 1 + count]
    all_rows, wholes = refs[1 + count], refs[2 + count : 2 + 2 * count]
    send, receive, row_send, row_receive = refs[2 + 2 * count :]
    me, t, m, core = position(top, mid)
    group = lax.axis_index("seq")
    greet(groups, top, mid)
    copies = {}

    def launch(a, key, source, slot, device):
        copies[(a,) + key] = remote(
            source, wholes[a].at[slot], send.at[(a,) + key], receive.at[(a,) + key], device
        )

    other = {"fsdp": slot_of(t, m, 1 - core, mid)}
    for a in range(count):
        for d in range(1, top):
            peer = {"fsdp": slot_of(lax.rem(t + d, top), m, core, mid)}
            launch(a, (d, 0, 0), shards[a], me, peer)
        for e in range(1, mid):
            peer = {"fsdp": slot_of(t, lax.rem(m + e, mid), core, mid)}
            launch(a, (0, e, 0), shards[a], me, peer)
        launch(a, (0, 0, 1), shards[a], me, other)
    for k in range(1, groups):
        copies[("rows", k)] = remote(
            rows,
            all_rows.at[group],
            row_send.at[k],
            row_receive.at[k],
            {"seq": lax.rem(group + k, groups)},
        )
    for a in range(count):
        wholes[a][me] = shards[a][...]
    all_rows[group] = rows[...]
    for a in range(count):
        for d in range(1, top):
            copies[(a, d, 0, 0)].wait_recv()
            slot = slot_of(lax.rem(t - d + top, top), m, core, mid)
            for e in range(1, mid):
                peer = {"fsdp": slot_of(t, lax.rem(m + e, mid), core, mid)}
                launch(a, (d, e, 0), wholes[a].at[slot], slot, peer)
            launch(a, (d, 0, 1), wholes[a].at[slot], slot, other)
    for a in range(count):
        for d in range(top):
            for e in range(1, mid):
                copies[(a, d, e, 0)].wait_recv()
                slot = slot_of(lax.rem(t - d + top, top), lax.rem(m - e + mid, mid), core, mid)
                launch(a, (d, e, 1), wholes[a].at[slot], slot, other)
    for key, copy in copies.items():
        copy.wait_send()
        if key[0] == "rows" or key[3] == 1:
            copy.wait_recv()


def gather_all(groups, shards, rows, arrays):
    top, mid = factors(shards)
    count = len(arrays)
    vmem = pl.BlockSpec(memory_space=pltpu.VMEM)
    out = [jax.ShapeDtypeStruct((groups,) + rows.shape, rows.dtype)]
    out += [jax.ShapeDtypeStruct((shards,) + array.shape, array.dtype) for array in arrays]
    return pl.pallas_call(
        functools.partial(gather_kernel, groups, top, mid, count),
        out_shape=out,
        in_specs=[vmem] * (1 + count),
        out_specs=[vmem] * (1 + count),
        scratch_shapes=[
            pltpu.SemaphoreType.DMA((count, top, mid, 2)),
            pltpu.SemaphoreType.DMA((count, top, mid, 2)),
            pltpu.SemaphoreType.DMA((groups,)),
            pltpu.SemaphoreType.DMA((groups,)),
        ],
        compiler_params=pltpu.CompilerParams(
            collective_id=0, has_side_effects=True, vmem_limit_bytes=VMEM_LIMIT
        ),
    )(rows, *arrays)


CHUNKS = 2


def add(left, right):
    return (left.astype(f32) + right.astype(f32)).astype(bf16)


def scatter_kernel(groups, top, mid, count, *refs):
    partial, flat, grads = refs[0], refs[1], refs[2 : 2 + count]
    refs = refs[2 + count :]
    summed, total, owned = refs[0], refs[1], refs[2 : 2 + count]
    refs = refs[2 + count :]
    pair = refs[:count]
    middle = refs[count : 2 * count]
    line = refs[2 * count : 3 * count]
    far = refs[3 * count : 4 * count]
    flat_pair, flat_mid, flat_top, flat_group, send, receive, flat_send, flat_receive, sum_sems = (
        refs[4 * count :]
    )
    me, t, m, core = position(top, mid)
    group = lax.axis_index("seq")
    greet(groups, top, mid)
    other = {"fsdp": slot_of(t, m, 1 - core, mid)}
    to_mid = [{"fsdp": slot_of(t, lax.rem(m + e, mid), core, mid)} for e in range(mid)]
    to_top = [{"fsdp": slot_of(lax.rem(t + d, top), m, core, mid)} for d in range(top)]
    to_group = [{"seq": lax.rem(group + k, groups)} for k in range(groups)]
    copies = []

    def launch(source, target, index, device):
        copy = remote(source, target, send.at[index], receive.at[index], device)
        copies.append(copy)
        return copy

    def launch_flat(stage, buffer, own, peers):
        started = []
        for k in range(1, len(peers)):
            copy = remote(
                buffer.at[own],
                buffer.at[own],
                flat_send.at[stage, k],
                flat_receive.at[stage, k],
                peers[k],
            )
            started.append(copy)
            copies.append(copy)
        return started

    def total_of(buffer, started):
        for copy in started:
            copy.wait_recv()
        value = buffer[0]
        for k in range(1, buffer.shape[0]):
            value = value + buffer[k]
        return value

    work = [(a, r) for a in range(count) for r in range(CHUNKS)]
    rows_of = [grads[a].shape[3] // CHUNKS for a in range(count)]

    def part(a, r):
        return pl.ds(r * rows_of[a], rows_of[a])

    flat_pair[core] = flat[...]
    stage_flat = launch_flat(0, flat_pair, core, [None, other])
    stage = {}
    for n, (a, r) in enumerate(work):
        stage[n] = launch(
            grads[a].at[:, :, 1 - core, part(a, r)], pair[a].at[:, :, part(a, r)], (n, 0), other
        )
    sums = []
    for k in range(1, groups):
        copy = remote(
            partial.at[lax.rem(group + k, groups)],
            summed.at[group],
            sum_sems.at[0, k],
            sum_sems.at[1, k],
            to_group[k],
        )
        sums.append(copy)
    summed[group] = partial[group]

    stage_mid = {}
    for n, (a, r) in enumerate(work):
        stage[n].wait_recv()

        @pl.loop(0, top)
        def _(i):
            for j in range(mid):
                at = part(a, r)
                pair[a][i, j, at] = add(pair[a][i, j, at], grads[a][i, j, core, at])

        for e in range(1, mid):
            stage_mid[n, e] = launch(
                pair[a].at[:, lax.rem(m + e, mid), part(a, r)],
                middle[a].at[e - 1, :, part(a, r)],
                (n, e),
                to_mid[e],
            )
        if n == 0:
            flat_mid[m] = total_of(flat_pair, stage_flat)
            stage_flat = launch_flat(1, flat_mid, m, to_mid)
    stage_top = {}
    for n, (a, r) in enumerate(work):
        for e in range(1, mid):
            stage_mid[n, e].wait_recv()

        @pl.loop(0, top)
        def _(i):
            at = part(a, r)
            value = pair[a][i, m, at].astype(f32)
            for e in range(1, mid):
                value = value + middle[a][e - 1, i, at].astype(f32)
            line[a][i, at] = value.astype(bf16)

        for d in range(1, top):
            stage_top[n, d] = launch(
                line[a].at[lax.rem(t + d, top), part(a, r)],
                far[a].at[d - 1, part(a, r)],
                (n, mid + d - 1),
                to_top[d],
            )
        if n == 0:
            flat_top[t] = total_of(flat_mid, stage_flat)
            stage_flat = launch_flat(2, flat_top, t, to_top)
    last = []
    for n, (a, r) in enumerate(work):
        at = part(a, r)
        for d in range(1, top):
            stage_top[n, d].wait_recv()
        value = line[a][t, at].astype(f32)
        for d in range(1, top):
            value = value + far[a][d - 1, at].astype(f32)
        owned[a][group, at] = value.astype(bf16)
        for k in range(1, groups):
            last.append(
                launch(
                    owned[a].at[group, at],
                    owned[a].at[group, at],
                    (n, mid + top - 2 + k),
                    to_group[k],
                )
            )
        if n == 0:
            flat_group[group] = total_of(flat_top, stage_flat)
            stage_flat = launch_flat(3, flat_group, group, to_group)
    total[...] = total_of(flat_group, stage_flat)
    for copy in last:
        copy.wait_recv()
    for copy in sums:
        copy.wait()
    for copy in copies:
        copy.wait_send()


def scatter_all(groups, shards, partial, flat, grads):
    top, mid = factors(shards)
    count = len(grads)
    vmem = pl.BlockSpec(memory_space=pltpu.VMEM)
    grads = [grad.reshape(top, mid, 2, grad.shape[0] // shards, grad.shape[1]) for grad in grads]
    shapes = [grad.shape[3:] for grad in grads]
    out = [
        jax.ShapeDtypeStruct(partial.shape, bf16),
        jax.ShapeDtypeStruct(flat.shape, f32),
    ] + [jax.ShapeDtypeStruct((groups,) + shape, bf16) for shape in shapes]
    most = max(2, mid, top, groups)
    stages = mid + top + groups - 2
    return pl.pallas_call(
        functools.partial(scatter_kernel, groups, top, mid, count),
        out_shape=out,
        in_specs=[vmem] * (2 + count),
        out_specs=[vmem] * (2 + count),
        scratch_shapes=[pltpu.VMEM((top, mid) + shape, bf16) for shape in shapes]
        + [pltpu.VMEM((max(1, mid - 1), top) + shape, bf16) for shape in shapes]
        + [pltpu.VMEM((top,) + shape, bf16) for shape in shapes]
        + [pltpu.VMEM((max(1, top - 1),) + shape, bf16) for shape in shapes]
        + [pltpu.VMEM((size,) + flat.shape, f32) for size in (2, mid, top, groups)]
        + [
            pltpu.SemaphoreType.DMA((count * CHUNKS, stages)),
            pltpu.SemaphoreType.DMA((count * CHUNKS, stages)),
            pltpu.SemaphoreType.DMA((4, most)),
            pltpu.SemaphoreType.DMA((4, most)),
            pltpu.SemaphoreType.DMA((2, groups)),
        ],
        compiler_params=pltpu.CompilerParams(
            collective_id=1, has_side_effects=True, vmem_limit_bytes=VMEM_LIMIT
        ),
    )(partial, flat, *grads)


def local(
    tokens,
    cotangent,
    documents,
    in_weight,
    kernel_taps,
    kernel_bias,
    step_bias,
    decay_log,
    skip_gain,
    pre_gain,
    norm_gain,
    out_weight,
):
    groups = lax.axis_size("seq")
    shards = lax.axis_size("fsdp")
    group = lax.axis_index("seq")
    heads = step_bias.shape[0]
    inner = norm_gain.shape[0]
    states = kernel_bias.shape[0] - inner
    half = inner // groups
    spread = out_weight.shape[0] % (HEAD_DIM * groups) == 0
    parts = shards if spread else 1

    def pick(array, axis):
        size = array.shape[axis]
        lead, tail = array.shape[:axis], array.shape[axis + 1 :]
        split = array.reshape(lead + (parts, groups, size // (parts * groups)) + tail)
        chosen = lax.dynamic_index_in_dim(split, group, axis + 1, keepdims=False)
        return chosen.reshape(lead + (size // groups,) + tail)

    def place(array):
        size = array.shape[-1] * groups
        lead = array.shape[:-1]
        split = array.reshape(lead + (parts, 1, size // (parts * groups)))
        blank = jnp.zeros(lead + (parts, groups, size // (parts * groups)), array.dtype)
        full = lax.dynamic_update_slice_in_dim(blank, split, group, len(lead) + 1)
        return full.reshape(lead + (size,))

    def unite(array):
        rows, width = array.shape[1:]
        split = array.reshape(groups, rows, parts, width // parts)
        return split.transpose(1, 2, 0, 3).reshape(rows, width * groups)

    conv_end = inner + inner + states
    conv_shard = jnp.concatenate(
        [
            pick(in_weight[:, inner : 2 * inner], 1),
            in_weight[:, 2 * inner : conv_end],
            pick(in_weight[:, conv_end:], 1),
        ],
        axis=1,
    )
    gate_shard = pick(in_weight[:, :inner], 1)
    out_rows = out_weight
    if spread:
        split = out_weight.reshape(groups, out_weight.shape[0] // groups, out_weight.shape[1])
        out_rows = lax.dynamic_index_in_dim(split, group, 0, keepdims=False)
    floats = tokens.astype(f32)
    normed_own = pre_norm(floats, pre_gain).astype(bf16)
    count, width = tokens.shape
    joined, conv_weight, gate_weight, out_part = gather_all(
        groups,
        shards,
        jnp.concatenate([normed_own, cotangent], axis=1),
        [conv_shard, gate_shard, out_rows],
    )
    joined = joined.reshape(groups * count, 2 * width)
    conv_weight = conv_weight.reshape(width, -1)
    gate_weight = gate_weight.reshape(width, -1)
    out_part = out_part.reshape(-1, width)
    if not spread:
        out_part = lax.dynamic_slice_in_dim(out_part, group * half, half, 0)
    normed_in, cot = joined[:, :width], joined[:, width:]

    projected = dot(normed_in, conv_weight).astype(bf16).astype(f32)
    segment = documents[0]
    taps = jnp.concatenate([pick(kernel_taps[:, :inner], 1), kernel_taps[:, inner:]], axis=1)
    tap_bias = jnp.concatenate([pick(kernel_bias[:inner], 0), kernel_bias[inner:]], axis=0)
    mixed, mixer_back = jax.vjp(
        lambda *given: mixer(segment, *given),
        projected[:, : half + states],
        projected[:, half + states :],
        taps,
        tap_bias,
        pick(step_bias, 0),
        pick(decay_log, 0),
        pick(skip_gain, 0),
    )
    gain = pick(norm_gain, 0)
    gates = dot(normed_in, gate_weight).astype(bf16).astype(f32)
    mixed = mixed.astype(bf16).astype(f32)
    back_normed = dot(cot, out_part, contract_rows)
    sigmoid = jax.nn.sigmoid(gates)
    silu = gates * sigmoid
    gated = mixed * silu
    back_gain = back_normed * gain
    sums = lax.psum(
        jnp.stack([jnp.sum(gated * gated, axis=1), jnp.sum(gated * back_gain, axis=1)]), "seq"
    )
    scale = lax.rsqrt(sums[0] / inner + norm_epsilon)
    unit = gated * scale[:, None]
    normed_bf = (unit * gain).astype(bf16)
    norm_gain_part = jnp.sum(back_normed * unit, axis=0)
    back_gated = scale[:, None] * (back_gain - unit * (scale * sums[1] / inner)[:, None])
    back_mixed = (back_gated * silu).astype(bf16).astype(f32)
    back_gates = (back_gated * mixed * sigmoid * (1.0 + gates * (1.0 - sigmoid))).astype(bf16)

    outward = dot(normed_bf, cot, contract_tokens).astype(bf16)
    gate_grad = dot(normed_in, back_gates, contract_tokens).astype(bf16)
    if not spread:
        blank = jnp.zeros((inner, width), bf16)
        outward = lax.dynamic_update_slice_in_dim(blank, outward, group * half, 0)
    branch = dot(normed_bf, out_part).astype(bf16)

    back_conv, back_steps, taps_part, bias_part, step_part, decay_part, skip_part = mixer_back(
        back_mixed
    )
    back_projected = jnp.concatenate([back_conv, back_steps], axis=1).astype(bf16)
    conv_grad = dot(normed_in, back_projected, contract_tokens).astype(bf16)
    back_in = dot(back_projected, conv_weight, contract_rows) + dot(
        back_gates, gate_weight, contract_rows
    )
    pre_gain_part = jnp.sum(back_in * normed_in.astype(f32), axis=0) / pre_gain

    pieces = (
        jnp.concatenate([place(taps_part[:, :half]), taps_part[:, half:]], axis=1),
        jnp.concatenate([place(bias_part[:half]), bias_part[half:]], axis=0),
        place(step_part),
        place(decay_part),
        place(skip_part),
        pre_gain_part,
        place(norm_gain_part),
    )
    flat = jnp.concatenate([piece.reshape(-1) for piece in pieces])
    padded = jnp.pad(flat, (0, -flat.size % 1024)).reshape(-1, 128)
    partial = jnp.concatenate(
        [
            back_in.astype(bf16).reshape(groups, count, width),
            branch.reshape(groups, count, width),
        ],
        axis=1,
    )
    partial, padded, conv_all, gate_all, out_all = scatter_all(
        groups, shards, partial, padded, [conv_grad, gate_grad, outward]
    )
    partial = jnp.sum(partial.astype(f32), axis=0)
    block_output = (floats + partial[count:]).astype(bf16)
    _, pre_back = jax.vjp(lambda given: pre_norm(given, pre_gain), floats)
    tokens_grad = cotangent.astype(f32) + pre_back(partial[:count])[0]
    conv_all, gate_all, out_all = (
        conv_all.astype(f32),
        gate_all.astype(f32),
        out_all.astype(f32),
    )
    if spread:
        outward_grad = out_all.reshape(-1, width)
    else:
        outward_grad = jnp.sum(out_all, axis=0)
    inward_grad = jnp.concatenate(
        [
            unite(gate_all),
            unite(conv_all[:, :, :half]),
            jnp.sum(conv_all[:, :, half : half + states], axis=0),
            unite(conv_all[:, :, half + states :]),
        ],
        axis=1,
    )
    flat = padded.reshape(-1)
    totals = []
    start = 0
    for piece in pieces:
        totals.append(flat[start : start + piece.size].reshape(piece.shape))
        start += piece.size
    return (
        block_output,
        tokens_grad,
        inward_grad,
        totals[0],
        totals[1],
        totals[2],
        totals[3],
        totals[4],
        totals[5],
        totals[6],
        outward_grad,
    )


def solution(mesh):
    rows = P(("fsdp", "seq"), None)
    split = P("fsdp", None)
    return jax.shard_map(
        local,
        mesh=mesh,
        in_specs=(rows, rows, split, split) + (P(),) * 7 + (split,),
        out_specs=(rows, rows, split) + (P(),) * 7 + (split,),
        check_vma=False,
    )
```

profile of v0, /device:TPU:1, one launch (start us, length us, event | category | flops | bytes accessed | tf_op | source)
XLA Modules:
  0.0 233.0 jit_solution(1653569507043543539)
XLA Ops:
  0.7 1.2 fusion.29
  2.9 1.1 fusion.31
  4.0 1.8 pad_maximum_fusion.3.refs_0_
  7.1 3.3 %dynamic-slice_reduce_fusion = (bf16[64,16,64]{2,1,0:T(8,128)(2,1)S(1)}, bf16[64,16,64]{2,1,0:T(8,128)(2,1)S(1)}) fusion(bf16[64,16,2,64]{3,2,1,0:T(2,128)(2,1)S(1)} %reshape.424, s32[]{:T(128)S(6)} %select_n.50, bf16[64,16,2,64]{3,2,1,0:T(2,128)(2,1)S(1)} %reshape.420), kind=kLoop, calls=%fused_computation.90 | loop fusion | bytes 524292 | tf_op jit(solution)/shard_map/jit(dynamic_index_in_dim)/dynamic_slice | solution.py:429
  10.6 0.7 pad_maximum_fusion.6.refs_1_
  11.3 0.9 reshape.425.refs_2_
  12.9 57.2 %shard_map.203 = (bf16[2,128,2048]{2,1,0:T(8,128)(2,1)}, bf16[16,64,1296]{2,1,0:T(8,128)(2,1)}, bf16[16,64,1024]{2,1,0:T(8,128)(2,1)}, bf16[16,64,1024]{2,1,0:T(8,128)(2,1)}) custom-call(bf16[128,2048]{1,0:T(8,128)(2,1)} %pad_maximum_fusion.3.refs_0_, bf16[64,1296]{1,0:T(8,128)(2,1)} %pad_maximum_fusion.6.refs_1_, bf16[64,1024]{1,0:T(8,128)(2,1)} %reshape.425.refs_2_, ...), custom_call_target="tpu_custom_call" | custom-call | tf_op jit(solution)/shard_map/pallas_call | solution.py:196
  70.4 3.2 %fusion.7 = f32[256,1296]{0,1:T(8,128)S(1)} fusion(bf16[1024,1296]{1,0:T(8,128)(2,1)} %bitcast.155, bf16[256,2048]{1,0:T(8,128)(2,1)} %bitcast.141), kind=kOutput, calls=%fused_computation.13 | convolution fusion | flops 680140800 | bytes 4734976 | tf_op jit(solution)/shard_map/dot_general | solution.py:24
  74.9 1.2 slice.237
  76.1 1.2 slice.236
  77.6 4.7 %fusion.76 = (bf16[256,1280]{0,1:T(8,128)(2,1)S(1)}, f32[256,1280]{0,1:T(8,128)}, f32[256,1280]{0,1:T(8,128)}) fusion(f32[256]{0:T(256)S(1)} %get-tuple-element.83, f32[253,1280]{0,1:T(8,128)S(1)} %slice.238, f32[1280]{0:T(1024)S(1)} %get-tuple-element.36, f32[256]{0:T(256)S(1)} %pad_convert_fusion.1, f32[254,1280]{0,1:T(8,128)} %slice.237, ...), kind=kLoop, calls=%fused_computation.184 | loop fusion | flops 5242880 | bytes 8517632 | tf_op jit(solution)/shard_map/convert.23
  82.3 0.9 copy-done.19
  85.2 1.3 slice.241
  86.5 1.6 fusion.15
  88.2 1.1 bitcast_convert_fusion
  89.2 2.5 %copy.43 = f32[256,1024]{1,0:T(8,128)} copy(f32[256,1024]{0,1:T(8,128)} %bitcast_convert_fusion) | data formatting | bytes 2097152 | tf_op jit(solution)/shard_map/convert_element_type | solution.py:492
  91.8 3.5 %fusion.35 = f32[256,1024]{1,0:T(8,128)} fusion(bf16[1024,1024]{1,0:T(8,128)(2,1)} %bitcast.160, bf16[256,2048]{1,0:T(8,128)(2,1)} %bitcast.142), kind=kOutput, calls=%fused_computation.93 | convolution fusion | flops 536870912 | bytes 3670016 | tf_op jit(solution)/shard_map/dot_general | solution.py:24
  95.3 3.4 %multiply_reduce_fusion.7 = (f32[256]{0:T(256)S(1)}, f32[256]{0:T(256)S(1)}, bf16[256,1024]{1,0:T(8,128)(2,1)S(1)}) fusion(f32[256,1024]{1,0:T(8,128)} %copy.43, f32[256,1024]{1,0:T(8,128)} %fusion.35, f32[1024]{0:T(1024)S(1)} %mul.392, bf16[1024,1024]{1,0:T(8,128)(2,1)} %bitcast.158, bf16[256,2048]{1,0:T(8,128)(2,1)} %bitcast.143), kind=kOutput, calls=%fused_computation.69 | convolution fusion | flops 540016128 | bytes 5249024 | tf_op jit(solution)/shard_map/dot_general | solution.py:24
  98.7 4.1 %psum.7 = f32[2,256]{1,0:T(2,128)S(1)} all-reduce(f32[2,256]{1,0:T(2,128)S(1)} %pad_maximum_fusion.10), channel_id=1, replica_groups=mesh['seq'=2,'fsdp'=16] {'seq'}, use_global_device_ids=true, to_apply=%region_5.6 | all-reduce | flops 512 | bytes 4096 | tf_op jit(solution)/shard_map/psum | solution.py:498
  102.9 3.7 %convolution_convert_fusion.5 = bf16[256,1024]{1,0:T(8,128)(2,1)} fusion(bf16[1024,1024]{1,0:T(8,128)(2,1)} %bitcast.161, f32[256]{0:T(256)S(1)} %bitcast.174, f32[1024]{0:T(1024)S(1)} %mul.392, f32[256,1024]{1,0:T(8,128)} %copy.43, bf16[256,1024]{1,0:T(8,128)(2,1)S(1)} %get-tuple-element.72), kind=kOutput, calls=%fused_computation.45 | convolution fusion | flops 539492352 | bytes 4199424 | tf_op jit(solution)/shard_map/dot_general | solution.py:24
  106.6 2.9 %multiply_convert_fusion.12 = (bf16[256,1024]{1,0:T(8,128)(2,1)}, bf16[256,1024]{1,0:T(8,128)(2,1)S(1)}, f32[1024]{0:T(1024)S(1)}) fusion(f32[256]{0:T(256)S(1)} %multiply_multiply_fusion, f32[256,1024]{1,0:T(8,128)S(1)} %copy-done.6, f32[256]{0:T(256)S(1)} %bitcast.176, f32[1024]{0:T(1024)S(1)} %mul.392, bf16[256,1024]{1,0:T(8,128)(2,1)} %copy-done.23, ...), kind=kLoop, calls=%fused_computation.66 | loop fusion | flops 5766144 | bytes 3680256 | tf_op jit(solution)/shard_map/convert_element_type | solution.py:506
  109.5 1.8 fusion.81
  111.3 2.0 copy.44
  113.3 3.8 %fusion.21 = (f32[16,256]{1,0:T(8,128)S(1)}, bf16[16,256,64]{1,2,0:T(8,128)(2,1)}) fusion(f32[256,1280]{0,1:T(8,128)} %get-tuple-element.52, bf16[16,256,64]{1,2,0:T(8,128)(2,1)} %bitcast.138, f32[256,256]{1,0:T(8,128)} %copy-done.29, f32[16,256]{1,0:T(8,128)S(1)} %copy_bitcast_fusion, pred[256,256]{1,0:T(8,128)(4,1)} %copy-done.33), kind=kOutput, calls=%fused_computation.55 | convolution fusion | flops 140505088 | bytes 2473984 | tf_op jit(solution)/shard_map/transpose(jvp(hij,hjp->hip))/dot_general | solution.py:33
  117.1 3.9 %fusion.6 = (f32[16,256]{1,0:T(8,128)S(1)}, f32[16,256]{1,0:T(8,128)S(1)}, bf16[256,256]{1,0:T(8,128)(2,1)}) fusion(f32[256,256]{1,0:T(8,128)S(1)} %copy-done.30, f32[16,256]{1,0:T(8,128)S(1)} %copy_bitcast_fusion, pred[256,256]{1,0:T(8,128)(4,1)S(1)} %copy-done.34, bf16[16,256,64]{1,2,0:T(8,128)(2,1)S(1)} %bitcast.139, f32[16,256,64]{1,2,0:T(8,128)S(1)} %bitcast.151, ...), kind=kOutput, calls=%fused_computation.11 | convolution fusion | flops 148299776 | bytes 2097152 | tf_op jit(solution)/shard_map/transpose(jvp(hij,hjp->hip))/dot_general | solution.py:33
  120.9 2.5 %reduce-window.16 = f32[16,2,128]{2,0,1:T(8,128)S(1)} reduce-window(f32[16,2,128]{2,0,1:T(8,128)S(1)} %copy_bitcast_fusion.1, f32[]{:T(128)} %constant.81.clone.1), window={size=1x1x128 pad=0_0x0_0x0_127}, to_apply=%region_10.11 | reduce-window | flops 520192 | bytes 32772 | tf_op jit(solution)/shard_map/reduce-window.2
  123.6 1.4 fusion.73
  125.0 1.6 fusion.17
  126.6 1.0 convolution_convert_fusion.7
  127.6 1.0 convolution_convert_fusion.8
  128.6 0.8 multiply_reduce_fusion.3
  130.3 1.3 multiply_reduce_fusion.2
  134.5 1.2 copy-done.15
  136.0 1.1 multiply_reduce_fusion.5
  137.1 1.0 pad_maximum_fusion.1.refs_0_
  141.0 2.1 convolution_convert_fusion
  143.1 3.1 %copy.51 = bf16[1024,1296]{1,0:T(8,128)(2,1)} copy(bf16[1024,1296]{0,1:T(8,128)(2,1)S(1)} %convolution_convert_fusion) | data formatting | bytes 5308416 | tf_op jit(solution)/shard_map/convert_element_type | solution.py:520
  146.2 3.3 %convolution_convert_fusion.3 = bf16[1024,1024]{1,0:T(8,128)(2,1)} fusion(bf16[256,1024]{1,0:T(8,128)(2,1)S(1)} %get-tuple-element.55, bf16[256,2048]{1,0:T(8,128)(2,1)} %bitcast.145), kind=kOutput, calls=%fused_computation.19 | convolution fusion | flops 537919488 | bytes 3145728 | tf_op jit(solution)/shard_map/dot_general | solution.py:24
  149.5 2.4 %convolution_convert_fusion.2 = bf16[1024,1024]{1,0:T(8,128)(2,1)} fusion(bf16[256,2048]{1,0:T(8,128)(2,1)S(1)} %bitcast.147, f32[256]{0:T(256)S(1)} %bitcast.177, f32[1024]{0:T(1024)S(1)} %mul.392, f32[256,1024]{1,0:T(8,128)S(1)} %copy-done.10, bf16[256,1024]{1,0:T(8,128)(2,1)S(1)} %copy-done.24), kind=kOutput, calls=%fused_computation.18 | convolution fusion | flops 540278784 | bytes 4199424 | tf_op jit(solution)/shard_map/dot_general | solution.py:24
  151.8 68.7 %shard_map.204 = (bf16[2,256,1024]{2,1,0:T(8,128)(2,1)}, f32[120,128]{1,0:T(8,128)}, bf16[2,64,1296]{2,1,0:T(8,128)(2,1)}, bf16[2,64,1024]{2,1,0:T(8,128)(2,1)}, bf16[2,64,1024]{2,1,0:T(8,128)(2,1)}) custom-call(bf16[2,256,1024]{2,1,0:T(8,128)(2,1)} %pad_maximum_fusion.1.refs_0_, f32[120,128]{1,0:T(8,128)} %pad_bitcast_fusion.refs_1_, ...), custom_call_target="tpu_custom_call" | custom-call | tf_op jit(solution)/shard_map/pallas_call | solution.py:378
  220.6 1.6 convert_reduce_fusion
  222.4 1.1 fusion.28
  224.1 0.8 copy.53
  224.9 1.0 reshape.471
  226.1 0.8 copy.52
  227.0 1.0 reshape.480
  227.9 1.1 pad_maximum_fusion
  232.2 0.9 bitcast_convert_fusion.1
  (216 shorter events, 18.2 us)
Async XLA Ops:
  0.6 11.5 %copy-start = (bf16[128,1024]{1,0:T(8,128)(2,1)S(1)}, bf16[128,1024]{1,0:T(8,128)(2,1)}, u32[]{:S(2)}) copy-start(bf16[128,1024]{1,0:T(8,128)(2,1)} %param.23) | copy-start | bytes 786436
  0.7 5.1 %slice-start = ((bf16[64,4384]{1,0:T(8,128)(2,1)}), bf16[64,32]{1,0:T(8,128)(2,1)S(1)}, s32[]{:S(2)}) async-start(bf16[64,4384]{1,0:T(8,128)(2,1)} %param.15), calls=%async_computation | async-start | bytes 32768 | tf_op jit(solution)/shard_map/slice | solution.py:450
  0.7 5.3 %copy-start.22 = (bf16[64,4384]{1,0:T(8,128)(2,1)S(1)}, bf16[64,4384]{1,0:T(8,128)(2,1)}, u32[]{:S(2)}) copy-start(bf16[64,4384]{1,0:T(8,128)(2,1)} %param.15) | copy-start | bytes 1683460
  6.5 4.1 %slice-start.1 = ((bf16[64,4384]{1,0:T(8,128)(2,1)}), bf16[64,256]{1,0:T(8,128)(2,1)S(1)}, s32[]{:S(2)}) async-start(bf16[64,4384]{1,0:T(8,128)(2,1)} %param.15), calls=%async_computation.1 | async-start | bytes 65536 | tf_op jit(solution)/shard_map/slice | solution.py:449
  10.4 59.7 %copy-start.32 = (s32[1,256]{1,0:T(1,128)S(1)}, s32[1,256]{1,0:T(1,128)}, u32[]{:S(2)}) copy-start(s32[1,256]{1,0:T(1,128)} %param.14) | copy-start | bytes 3076
  74.9 2.7 %copy-start.38 = (f32[256]{0:T(256)}, f32[256]{0:T(256)S(1)}, u32[]{:S(2)}) copy-start(f32[256]{0:T(256)S(1)} %pad_convert_fusion.1) | copy-start | bytes 3076
  76.0 1.3 copy-start.36
  76.0 1.3 slice-start.5
  76.0 1.5 slice-start.4
  77.6 5.8 %copy-start.46 = (f32[32]{0:T(128)S(1)}, f32[32]{0:T(128)}, u32[]{:S(2)}) copy-start(f32[32]{0:T(128)} %param.20) | copy-start | bytes 388
  77.6 5.9 %copy-start.47 = (f32[32]{0:T(128)S(1)}, f32[32]{0:T(128)}, u32[]{:S(2)}) copy-start(f32[32]{0:T(128)} %param.19) | copy-start | bytes 388
  77.6 6.2 %copy-start.48 = (f32[32]{0:T(128)S(1)}, f32[32]{0:T(128)}, u32[]{:S(2)}) copy-start(f32[32]{0:T(128)} %param.18) | copy-start | bytes 388
  83.4 4.7 %copy-start.29 = (f32[256,256]{1,0:T(8,128)}, f32[256,256]{1,0:T(8,128)S(1)}, u32[]{:S(2)}) copy-start(f32[256,256]{1,0:T(8,128)S(1)} %fusion.44) | copy-start | bytes 786436
  83.8 4.3 %copy-start.42 = (f32[16]{0:T(128)}, f32[16]{0:T(128)S(1)}, u32[]{:S(2)}) copy-start(f32[16]{0:T(128)S(1)} %get-tuple-element.80) | copy-start | bytes 196
  84.1 4.0 %copy-start.37 = (f32[16]{0:T(128)}, f32[16]{0:T(128)S(1)}, u32[]{:S(2)}) copy-start(f32[16]{0:T(128)S(1)} %dynamic-slice_reduce_fusion.6) | copy-start | bytes 196
  85.2 3.0 %copy-start.33 = (pred[256,256]{1,0:T(8,128)(4,1)}, pred[256,256]{1,0:T(8,128)(4,1)S(1)}, u32[]{:S(2)}) copy-start(pred[256,256]{1,0:T(8,128)(4,1)S(1)} %fusion.42) | copy-start | bytes 196612
  86.5 1.6 copy-start.11
  98.7 7.9 %copy-start.23 = (bf16[256,1024]{1,0:T(8,128)(2,1)}, bf16[256,1024]{1,0:T(8,128)(2,1)S(1)}, u32[]{:S(2)}) copy-start(bf16[256,1024]{1,0:T(8,128)(2,1)S(1)} %get-tuple-element.72) | copy-start | bytes 1572868
  102.9 3.7 %copy-start.6 = (f32[256,1024]{1,0:T(8,128)S(1)}, f32[256,1024]{1,0:T(8,128)}, u32[]{:S(2)}) copy-start(f32[256,1024]{1,0:T(8,128)} %fusion.35) | copy-start | bytes 3145732
  102.9 3.7 %copy-start.9 = (f32[256,1024]{1,0:T(8,128)S(1)}, f32[256,1024]{1,0:T(8,128)}, u32[]{:S(2)}) copy-start(f32[256,1024]{1,0:T(8,128)} %copy.43) | copy-start | bytes 3145732
  106.6 2.9 %copy-start.18 = (bf16[16,64,1024]{2,1,0:T(8,128)(2,1)S(1)}, bf16[16,64,1024]{2,1,0:T(8,128)(2,1)}, u32[]{:S(2)}) copy-start(bf16[16,64,1024]{2,1,0:T(8,128)(2,1)} %get-tuple-element.22) | copy-start | bytes 6291460
  113.3 3.8 %copy-start.4 = (bf16[256,1024]{0,1:T(8,128)(2,1)S(1)}, bf16[256,1024]{0,1:T(8,128)(2,1)}, u32[]{:S(2)}) copy-start(bf16[256,1024]{0,1:T(8,128)(2,1)} %copy.44) | copy-start | bytes 1572868
  113.3 3.8 %copy-start.12 = (f32[256,1024]{0,1:T(8,128)S(1)}, f32[256,1024]{0,1:T(8,128)}, u32[]{:S(2)}) copy-start(f32[256,1024]{0,1:T(8,128)} %copy-done.11) | copy-start | bytes 3145732
  113.3 3.8 %copy-start.30 = (f32[256,256]{1,0:T(8,128)S(1)}, f32[256,256]{1,0:T(8,128)}, u32[]{:S(2)}) copy-start(f32[256,256]{1,0:T(8,128)} %copy-done.29) | copy-start | bytes 786436
  113.3 3.8 %copy-start.34 = (pred[256,256]{1,0:T(8,128)(4,1)S(1)}, pred[256,256]{1,0:T(8,128)(4,1)}, u32[]{:S(2)}) copy-start(pred[256,256]{1,0:T(8,128)(4,1)} %copy-done.33) | copy-start | bytes 196612
  123.6 3.0 %copy-start.25 = (bf16[256,256]{1,0:T(8,128)(2,1)S(1)}, bf16[256,256]{1,0:T(8,128)(2,1)}, u32[]{:S(2)}) copy-start(bf16[256,256]{1,0:T(8,128)(2,1)} %get-tuple-element.31) | copy-start | bytes 393220
  125.0 3.6 %copy-start.3 = (f32[256,1280]{0,1:T(8,128)S(1)}, f32[256,1280]{0,1:T(8,128)}, u32[]{:S(2)}) copy-start(f32[256,1280]{0,1:T(8,128)} %get-tuple-element.53) | copy-start | bytes 3932164
  128.6 1.3 copy-start.1
  128.6 1.7 copy-start.2
  128.6 1.7 copy-start.39
  133.3 1.2 copy-start.7
  133.3 2.4 %copy-start.15 = (bf16[16,64,1296]{2,1,0:T(8,128)(2,1)S(1)}, bf16[16,64,1296]{2,1,0:T(8,128)(2,1)}, u32[]{:S(2)}) copy-start(bf16[16,64,1296]{2,1,0:T(8,128)(2,1)} %get-tuple-element.21) | copy-start | bytes 7962628
  133.3 2.6 %copy-start.20 = (f32[256,1024]{1,0:T(8,128)S(1)}, f32[256,1024]{1,0:T(8,128)}, u32[]{:S(2)}) copy-start(f32[256,1024]{1,0:T(8,128)} %fusion.81) | copy-start | bytes 3145732
  134.0 3.0 %copy-start.16 = (bf16[256,1280]{0,1:T(8,128)(2,1)}, bf16[256,1280]{0,1:T(8,128)(2,1)S(1)}, u32[]{:S(2)}) copy-start(bf16[256,1280]{0,1:T(8,128)(2,1)S(1)} %get-tuple-element.59) | copy-start | bytes 1966084
  137.1 2.1 copy-start.45
  137.1 2.4 %copy-start.5 = (bf16[256,1024]{0,1:T(8,128)(2,1)S(1)}, bf16[256,1024]{0,1:T(8,128)(2,1)}, u32[]{:S(2)}) copy-start(bf16[256,1024]{0,1:T(8,128)(2,1)} %copy.44) | copy-start | bytes 1572868
  137.1 2.4 %copy-start.13 = (f32[256,1024]{0,1:T(8,128)S(1)}, f32[256,1024]{0,1:T(8,128)}, u32[]{:S(2)}) copy-start(f32[256,1024]{0,1:T(8,128)} %copy-done.11) | copy-start | bytes 3145732
  138.1 1.9 copy-start.31
  146.2 3.3 %copy-start.8 = (bf16[2,128,2048]{2,1,0:T(8,128)(2,1)S(1)}, bf16[2,128,2048]{2,1,0:T(8,128)(2,1)}, u32[]{:S(2)}) copy-start(bf16[2,128,2048]{2,1,0:T(8,128)(2,1)} %get-tuple-element.20) | copy-start | bytes 3145732
  146.2 3.3 %copy-start.10 = (f32[256,1024]{1,0:T(8,128)S(1)}, f32[256,1024]{1,0:T(8,128)}, u32[]{:S(2)}) copy-start(f32[256,1024]{1,0:T(8,128)} %copy.43) | copy-start | bytes 3145732
  146.2 3.3 %copy-start.24 = (bf16[256,1024]{1,0:T(8,128)(2,1)S(1)}, bf16[256,1024]{1,0:T(8,128)(2,1)}, u32[]{:S(2)}) copy-start(bf16[256,1024]{1,0:T(8,128)(2,1)} %copy-done.23) | copy-start | bytes 1572868
  220.5 1.7 copy-start.14
  220.5 1.8 copy-start.44
  220.5 1.8 copy-start.21
  220.5 1.8 copy-start.41
  222.3 1.1 copy-start.17
  227.9 1.1 copy-start.35
  227.9 4.3 %copy-start.27 = (bf16[2,64,1024]{2,1,0:T(8,128)(2,1)S(1)}, bf16[2,64,1024]{2,1,0:T(8,128)(2,1)}, u32[]{:S(2)}) copy-start(bf16[2,64,1024]{2,1,0:T(8,128)(2,1)} %get-tuple-element.28) | copy-start | bytes 786436
  (7 other events, 5.7 us)
where the time goes:
time: 234 us; the launch traced here: 233 us
  Pallas kernels  126 us (54%)
  matrix products  35.8 us (15%)
  local copies, waits for them, and re-layouts  34.4 us (15%)
  other arithmetic  31.2 us (13%)
  blocking collectives  4.11 us (2%)
    pallas_call x1, Pallas kernels, scatter_all(): pl.pallas_call(functools.partial(scatter_kernel, groups, top, mid, count)...  68.7 us
    pallas_call x1, Pallas kernels, gather_all(): pl.pallas_call(functools.partial(gather_kernel, groups, top, mid, count),...  57.2 us
    dot_general x9, matrix products, dot(): return lax.dot_general(left, right, dims, preferred_element_type=f32)  24.4 us
    dot_general x6, matrix products, product(): jnp.einsum(spec, left.astype(bf16), right.astype(bf16), preferred_element...  11.4 us
    another operation x6, other arithmetic  7.91 us
    unnamed x99, local copies, waits for them, and re-layouts  4.98 us

commit v1 on v0

--- a/solution.py
+++ b/solution.py
@@ -398,7 +398,7 @@
     )(partial, flat, *grads)
 
 
-def local(
+def general(
     tokens,
     cotangent,
     documents,
@@ -587,6 +587,827 @@
     )
 
 
+LANES = 128
+FAR = -1e30
+exact = lax.Precision.HIGHEST
+
+
+def sharp(left, right, dims=(((1,), (0,)), ((), ()))):
+    return lax.dot_general(left, right, dims, precision=exact, preferred_element_type=f32)
+
+
+def iota(shape, axis):
+    return lax.broadcasted_iota(jnp.int32, shape, axis)
+
+
+def span_of(index, size):
+    return pl.ds(pl.multiple_of(index * size, size), size)
+
+
+class Courier:
+    def __init__(self, send):
+        self.send = send
+        self.count = 0
+        self.made = []
+
+    def start(self, source, target, receive, device, when=None):
+        slot = self.count
+        self.count += 1
+
+        def make():
+            return pltpu.make_async_remote_copy(
+                src_ref=source(),
+                dst_ref=target(),
+                send_sem=self.send.at[slot],
+                recv_sem=receive(),
+                device_id=device(),
+                device_id_type=MESH,
+            )
+
+        self.made.append((make, when))
+        self.run(lambda: make().start(), when)
+
+    def run(self, act, when):
+        if when is None:
+            act()
+        else:
+            pl.when(when)(act)
+
+    def arrive(self, target, receive, device):
+        pltpu.make_async_remote_copy(
+            src_ref=target,
+            dst_ref=target,
+            send_sem=self.send.at[0],
+            recv_sem=receive,
+            device_id=device,
+            device_id_type=MESH,
+        ).wait_recv()
+
+    def finish(self):
+        for make, when in self.made:
+            self.run(lambda make=make: make().wait_send(), when)
+
+
+def fused_kernel(top, *refs):
+    (
+        tokens, cotangent, documents, in_weight, taps, tap_bias, params, pre_gain, norm_gain, out_weight,
+        block_output, tokens_grad, in_grad, taps_grad, bias_grad, heads_grad, pre_grad, norm_grad, out_grad,
+        nall, call, docs, conv_pack, gate_pack, conv_all, gate_all, out_all,
+        proj, act, dact, mk, bias_mask, step, ldec, sgate, cum, cum_t, cum_b, step_e, skip_e, scaled,
+        scores, decay, weigh, inside, mixed, gates, bnorm, gain_own, sums, sums_all, totals,
+        normed_bf, bmixed, bgates, norm_part, part_b, part_i, dscore, x1, x2, dz, skip_part, bproj, pre_part,
+        gr_out, gr_gate, gr_conv, y_out, y_gate, y_conv, line_out, line_gate, line_conv,
+        low_out, low_gate, low_conv, high_out, high_gate, high_conv,
+        own_out, own_gate, own_conv, flat, flat_y, flat_z, flat_all, got_b, got_i,
+        send, r_rows, r_docs, r_conv, r_gate, r_out, r_sums, r_part,
+        ry_out, ry_gate, ry_conv, rl_out, rl_gate, rl_conv, rh_out, rh_gate, rh_conv,
+        ro_out, ro_gate, ro_conv, r_flat,
+    ) = refs
+    mid = 2
+    me, t, m, c = position(top, mid)
+    g = lax.axis_index("seq")
+    count, width = tokens.shape
+    length = documents.shape[1]
+    seqs = 2
+    total = seqs * length
+    rows = in_weight.shape[0]
+    inner = norm_gain.shape[1]
+    quarter = inner // 4
+    tiles = quarter // LANES
+    states = taps.shape[1] - inner
+    conv_tiles = tiles + states // LANES
+    active = conv_tiles * LANES
+    conv_cols = active + LANES
+    heads = params_heads(inner)
+    local_heads = heads // 4
+    mail = Courier(send)
+
+    def dev(tt, mm, cc):
+        return lambda: {"fsdp": slot_of(tt, mm, cc, mid)}
+
+    def dev_g(gg, tt, mm, cc):
+        return lambda: {"seq": gg, "fsdp": slot_of(tt, mm, cc, mid)}
+
+    here = {"fsdp": slot_of(t, m, 1 - c, mid)}
+    group = [
+        (2 * (1 - c) + g, dev_g(g, t, m, 1 - c)),
+        (2 * c + 1 - g, dev_g(1 - g, t, m, c)),
+        (2 * (1 - c) + 1 - g, dev_g(1 - g, t, m, 1 - c)),
+    ]
+    mine = 2 * c + g
+
+    barrier = pltpu.get_barrier_semaphore()
+    greeted = [d() for _, d in group]
+    greeted += [{"fsdp": slot_of(t, 1 - m, cc, mid)} for cc in range(2)]
+    greeted += [
+        {"fsdp": slot_of(lax.rem(t + d, top), m, cc, mid)} for d in range(1, top) for cc in range(2)
+    ]
+    for peer in greeted:
+        pl.semaphore_signal(barrier, inc=1, device_id=peer, device_id_type=MESH)
+
+    def tile_of(n, cc):
+        return 4 * n + 2 * cc + g
+
+    def selector(cc):
+        glob, loc = iota((LANES, LANES), 0), iota((LANES, LANES), 1)
+        wanted = 8 * (loc // 2) + 4 * cc + 2 * g + loc % 2
+        return jnp.where((glob == wanted) & (loc < local_heads), 1.0, 0.0)
+
+    def pack(conv, gate, cc):
+        for n in range(tiles):
+            at = span_of(tile_of(n, cc) + inner // LANES, LANES)
+            conv[:, n * LANES : (n + 1) * LANES] = in_weight[:, at]
+        conv[:, quarter:active] = in_weight[:, 2 * inner : 2 * inner + states]
+        picked = dot(in_weight[:, 2 * inner + states :], selector(cc)[:heads].astype(bf16))
+        conv[:, active:] = picked.astype(bf16)
+
+    def pack_gate(gate, cc):
+        for n in range(tiles):
+            gate[:, n * LANES : (n + 1) * LANES] = in_weight[:, span_of(tile_of(n, cc), LANES)]
+
+    pack(conv_all.at[me], None, c)
+    pack(conv_pack, None, 1 - c)
+    pl.semaphore_wait(barrier, len(greeted))
+
+    def spread(mine_ref, pack_ref, all_ref, receive):
+        for src, cc in ((mine_ref, c), (lambda: pack_ref, 1 - c)):
+            for up in (1, -1):
+                ok = (t + 1 < top) if up == 1 else (t >= 1)
+                mail.start(
+                    src, lambda: all_ref.at[me], lambda: receive.at[me],
+                    dev(t + up, m, cc), ok,
+                )
+            mail.start(
+                src, lambda: all_ref.at[me], lambda: receive.at[me], dev(t, 1 - m, cc)
+            )
+        mail.start(lambda: pack_ref, lambda: all_ref.at[me], lambda: receive.at[me], dev(t, m, 1 - c))
+
+    def relay(all_ref, receive, d):
+        for up in (1, -1):
+            ok = (t >= d) if up == 1 else (t + d < top)
+            onward = ok & ((t + 1 < top) if up == 1 else (t >= 1))
+            from_t = jnp.clip(t - up * d, 0, top - 1)
+            for cc in range(2):
+                slot = slot_of(from_t, m, cc, mid)
+                mail.run(lambda slot=slot: mail.arrive(all_ref.at[slot], receive.at[slot], here), ok)
+                block = lambda slot=slot: all_ref.at[slot]
+                sem = lambda slot=slot: receive.at[slot]
+                mail.start(block, block, sem, dev(t + up, m, c), onward)
+                mail.start(block, block, sem, dev(t, 1 - m, c), ok)
+
+    def settle(all_ref, receive):
+        slot = slot_of(t, m, 1 - c, mid)
+        mail.arrive(all_ref.at[slot], receive.at[slot], here)
+        for tt in range(top):
+            for cc in range(2):
+                slot = slot_of(tt, 1 - m, cc, mid)
+                mail.arrive(all_ref.at[slot], receive.at[slot], here)
+
+    spread(lambda: conv_all.at[me], conv_pack, conv_all, r_conv)
+
+    floats = tokens[...].astype(f32)
+    nall[mine] = pre_norm(floats, pre_gain[...]).astype(bf16)
+    for k, (_, device) in enumerate(group):
+        mail.start(lambda: nall.at[mine], lambda: nall.at[mine], lambda: r_rows.at[0, mine], device)
+    docs[c] = jnp.broadcast_to(documents[...].astype(f32), (8, length))
+    mail.start(lambda: docs.at[c], lambda: docs.at[c], lambda: r_docs.at[0], dev(t, m, 1 - c))
+
+    pack_gate(gate_all.at[me], c)
+    pack_gate(gate_pack, 1 - c)
+    relay(conv_all, r_conv, 1)
+    spread(lambda: gate_all.at[me], gate_pack, gate_all, r_gate)
+
+    holder = c == g
+    keeper = c == m
+    mail.run(lambda: out_all.__setitem__(t, out_weight[...]), holder & keeper)
+    row_block = lambda: out_weight
+    row_target = lambda: out_all.at[t]
+    row_sem = lambda: r_out.at[t]
+    mail.start(row_block, row_target, row_sem, dev(t + 1, m, m), holder & (t + 1 < top))
+    mail.start(row_block, row_target, row_sem, dev(t - 1, m, m), holder & (t >= 1))
+    mail.start(row_block, row_target, row_sem, dev(t, 1 - m, m), holder)
+    mail.start(row_block, row_target, row_sem, dev(t, m, 1 - c), holder & (c != m))
+
+    def relay_rows(d):
+        for up in (1, -1):
+            ok = keeper & ((t >= d) if up == 1 else (t + d < top))
+            onward = ok & ((t + 1 < top) if up == 1 else (t >= 1))
+            slot = jnp.clip(t - up * d, 0, top - 1)
+            mail.run(lambda: mail.arrive(out_all.at[slot], r_out.at[slot], here), ok)
+            block = lambda slot=slot: out_all.at[slot]
+            sem = lambda slot=slot: r_out.at[slot]
+            mail.start(block, block, sem, dev(t + up, m, c), onward)
+            mail.start(block, block, sem, dev(t, 1 - m, c), ok)
+
+    def settle_rows():
+        mail.run(lambda: mail.arrive(out_all.at[t], r_out.at[t], here), keeper & (c != g))
+        for tt in range(top):
+            mail.run(lambda tt=tt: mail.arrive(out_all.at[tt], r_out.at[tt], here), c != m)
+
+    call[mine] = cotangent[...]
+    for k, (_, device) in enumerate(group):
+        mail.start(lambda: call.at[mine], lambda: call.at[mine], lambda: r_rows.at[1, mine], device)
+
+    for slot, _ in group:
+        mail.arrive(nall.at[slot], r_rows.at[0, slot], here)
+    mail.arrive(docs.at[1 - c], r_docs.at[0], here)
+
+    @pl.loop(0, seqs)
+    def _(s):
+        row = docs[s][:1]
+        column = jnp.broadcast_to(row, (LANES, length)).T
+        wide = jnp.concatenate([column] * (length // LANES), axis=1)
+        ahead = iota((length, length), 0) >= iota((length, length), 1)
+        bias_mask[s] = jnp.where(ahead & (wide == row), 0.0, FAR)
+        place = iota((length, LANES), 0)
+        for k in range(1, CONV):
+            same = (pltpu.roll(column, k, 0) == column) & (place >= k)
+            mk[s, k - 1] = jnp.where(same, 1.0, 0.0)
+
+    for n in range(tiles):
+        gain_own[:, n * LANES : (n + 1) * LANES] = norm_gain[:, span_of(tile_of(n, c), LANES)]
+
+    for d in range(2, top):
+        relay(conv_all, r_conv, d)
+    settle(conv_all, r_conv)
+
+    def tall(ref):
+        return ref[...].reshape(total, width)
+
+    def weights(ref, cols):
+        return ref[:, :, cols].reshape(width, cols.size)
+
+    wide_cols = 256
+
+    @pl.loop(0, conv_cols // wide_cols)
+    def _(n):
+        at = span_of(n, wide_cols)
+        proj[:, at] = dot(tall(nall), weights(conv_all, at)).astype(bf16)
+
+    if conv_cols % wide_cols:
+        rest = pl.ds(conv_cols - LANES, LANES)
+        proj[:, rest] = dot(tall(nall), weights(conv_all, rest)).astype(bf16)
+
+    relay(gate_all, r_gate, 1)
+    relay_rows(1)
+
+    chosen = sharp(params[...], selector(c))
+    rate = jnp.exp(chosen[1:2])
+    raw = proj[:, active:].astype(f32) + chosen[:1]
+    step[...] = jnp.maximum(raw, 0.0) + jnp.log1p(jnp.exp(-jnp.abs(raw)))
+    sgate[...] = jax.nn.sigmoid(raw)
+    ldec[...] = step[...] * -rate
+    to_channels = jnp.where(iota((LANES, quarter), 1) // HEAD_DIM == iota((LANES, quarter), 0), 1.0, 0.0)
+    to_heads = jnp.where(iota((quarter, LANES), 0) // HEAD_DIM == iota((quarter, LANES), 1), 1.0, 0.0)
+    step_e[...] = sharp(step[...], to_channels)
+    skip_e[...] = sharp(chosen, to_channels)
+    lower = jnp.where(iota((length, length), 0) >= iota((length, length), 1), 1.0, 0.0)
+    for s in range(seqs):
+        at = slice(s * length, (s + 1) * length)
+        cum[at] = sharp(lower, ldec[at])
+        cum_t[s] = cum[at].T
+    for h in range(local_heads):
+        cum_b[h] = jnp.broadcast_to(cum[:, h : h + 1], (total, LANES))
+
+    def conv_tile(n):
+        return jnp.where(n < tiles, tile_of(n, c), n - tiles + inner // LANES)
+
+    @pl.loop(0, seqs * conv_tiles)
+    def _(i):
+        s, n = i // conv_tiles, i % conv_tiles
+        at, cols = span_of(s, length), span_of(n, LANES)
+        where = span_of(conv_tile(n), LANES)
+        x = proj[at, cols].astype(f32)
+        tap = taps[:, where]
+        z = tap_bias[:, where] + x * tap[CONV - 1 : CONV]
+        for k in range(1, CONV):
+            z = z + tap[CONV - 1 - k : CONV - k] * (pltpu.roll(x, k, 0) * mk[s, k - 1])
+        sig = jax.nn.sigmoid(z)
+        act[at, cols] = z * sig
+        dact[at, cols] = sig * (1.0 + z * (1.0 - sig))
+
+    relay(gate_all, r_gate, 2)
+    relay_rows(2)
+
+    def matrices(s):
+        at = span_of(s, length)
+        return (
+            act[at, quarter : quarter + STATE].astype(bf16),
+            act[at, quarter + STATE : active].astype(bf16),
+        )
+
+    @pl.loop(0, seqs)
+    def _(s):
+        b_in, c_out = matrices(s)
+        scores[s] = dot(c_out, b_in, contract_rows)
+
+    half_of = lambda: iota((length, LANES), 1) // HEAD_DIM
+
+    @pl.loop(0, seqs * tiles)
+    def _(i):
+        s, n = i // tiles, i % tiles
+        at, cols = span_of(s, length), span_of(n, LANES)
+        vals = act[at, cols]
+        sc = (vals * step_e[at, cols]).astype(bf16)
+        scaled[at, cols] = sc
+        y = jnp.zeros((length, LANES), f32)
+        for b in range(2):
+            h = 2 * n + b
+            col = cum_b[h, at]
+            gap = jnp.concatenate([col] * (length // LANES), axis=1) - cum_t[s, pl.ds(h, 1)]
+            d = jnp.exp(gap + bias_mask[s])
+            decay[s * local_heads + h] = d
+            w = (d * scores[s]).astype(bf16)
+            weigh[s * local_heads + h] = w
+            y = y + dot(w, jnp.where(half_of() == b, sc, jnp.zeros_like(sc)))
+        inside[at, cols] = y
+        mixed[at, cols] = (y + vals * skip_e[2:3, cols]).astype(bf16)
+
+    for d in range(3, top):
+        relay(gate_all, r_gate, d)
+        relay_rows(d)
+    settle(gate_all, r_gate)
+
+    @pl.loop(0, quarter // wide_cols)
+    def _(n):
+        at = span_of(n, wide_cols)
+        gates[:, at] = dot(tall(nall), weights(gate_all, at)).astype(bf16)
+
+    settle_rows()
+    for slot, _ in group:
+        mail.arrive(call.at[slot], r_rows.at[1, slot], here)
+
+    @pl.loop(0, tiles // 2)
+    def _(n):
+        w = out_all[pl.ds(2 * n, 2)].reshape(2 * LANES, width)
+        bnorm[:, span_of(n, 2 * LANES)] = dot(tall(call), w, contract_rows)
+
+    strip = 64
+
+    @pl.loop(0, total // strip)
+    def _(i):
+        at = span_of(i, strip)
+        gate = gates[at].astype(f32)
+        gated = mixed[at].astype(f32) * (gate * jax.nn.sigmoid(gate))
+        first = jnp.sum(gated * gated, axis=1, keepdims=True)
+        second = jnp.sum(gated * (bnorm[at] * gain_own[...]), axis=1, keepdims=True)
+        lane = iota((strip, LANES), 1)
+        sums[at] = jnp.where(lane == 0, first, jnp.where(lane == 1, second, 0.0))
+
+    sums_all[mine] = sums[...].T[:8]
+    for k, (_, device) in enumerate(group):
+        mail.start(lambda: sums_all.at[mine], lambda: sums_all.at[mine], lambda: r_sums.at[mine], device)
+    for slot, _ in group:
+        mail.arrive(sums_all.at[slot], r_sums.at[slot], here)
+    summed = (sums_all[0] + sums_all[1]) + (sums_all[2] + sums_all[3])
+    totals[...] = jnp.concatenate([summed, jnp.zeros((LANES - 8, total), f32)], axis=0).T
+
+    norm_part[...] = jnp.zeros_like(norm_part)
+
+    @pl.loop(0, total // strip)
+    def _(i):
+        at = span_of(i, strip)
+        gate = gates[at].astype(f32)
+        mix = mixed[at].astype(f32)
+        sig = jax.nn.sigmoid(gate)
+        silu = gate * sig
+        gated = mix * silu
+        gain = gain_own[...]
+        scale = lax.rsqrt(totals[at, 0:1] / inner + norm_epsilon)
+        unit = gated * scale
+        back = bnorm[at]
+        normed_bf[at] = (unit * gain).astype(bf16)
+        norm_part[...] += jnp.sum(back * unit, axis=0, keepdims=True)
+        back_gated = scale * (back * gain - unit * (scale * totals[at, 1:2] / inner))
+        bmixed[at] = (back_gated * silu).astype(bf16)
+        bgates[at] = (back_gated * mix * sig * (1.0 + gate * (1.0 - sig))).astype(bf16)
+
+    def tall_cols(ref, at):
+        return ref[:, :, at].reshape(total, at.size)
+
+    order = []
+    for k in range(top // 2):
+        order += [top - 1 - k, k]
+
+    for tt in order:
+        cols = slice(tt * LANES, (tt + 1) * LANES)
+        gr_out[tt] = dot(normed_bf[:, cols], tall(call), contract_tokens).astype(bf16)
+        mail.start(
+            lambda tt=tt: gr_out.at[tt], lambda tt=tt: y_out.at[tt], lambda tt=tt: ry_out.at[tt],
+            dev(t, 1 - m, c), c != m,
+        )
+
+    block = width // top
+    for tt in order:
+        got = dot(tall_cols(nall, pl.ds(tt * block, block)), bgates[...], contract_tokens).astype(bf16)
+        gr_gate[tt] = got.reshape(gr_gate.shape[1:])
+        mail.start(
+            lambda tt=tt: gr_gate.at[tt, 1 - m], lambda tt=tt: y_gate.at[tt], lambda tt=tt: ry_gate.at[tt],
+            dev(t, 1 - m, c),
+        )
+
+    @pl.loop(0, width // wide_cols)
+    def _(n):
+        at = span_of(n, wide_cols)
+        w = out_all[:, :, at].reshape(quarter, wide_cols)
+        part_b[:, :, at] = dot(normed_bf[...], w).astype(bf16).reshape(4, count, wide_cols)
+
+    for slot, device in group:
+        mail.start(
+            lambda slot=slot: part_b.at[slot], lambda: got_b.at[mine], lambda: r_part.at[0, mine], device
+        )
+
+    skip_part[...] = jnp.zeros_like(skip_part)
+    dscore[...] = jnp.zeros_like(dscore)
+
+    @pl.loop(0, seqs * tiles)
+    def _(i):
+        s, n = i // tiles, i % tiles
+        at, cols = span_of(s, length), span_of(n, LANES)
+        back = bmixed[at, cols]
+        sc = scaled[at, cols]
+        ds = jnp.zeros((length, LANES), f32)
+        gather = dscore[s]
+        for b in range(2):
+            h = s * local_heads + 2 * n + b
+            one = jnp.where(half_of() == b, back, jnp.zeros_like(back))
+            gather = gather + decay[h] * dot(one, sc, contract_rows)
+            ds = ds + dot(weigh[h], one, contract_tokens)
+        dscore[s] = gather
+        back = back.astype(f32)
+        vals = act[at, cols]
+        x1[at, cols] = back * inside[at, cols] - sc.astype(f32) * ds
+        x2[at, cols] = ds * vals
+        dz[at, cols] = (back * skip_e[2:3, cols] + ds * step_e[at, cols]) * dact[at, cols]
+        skip_part[:, cols] += jnp.sum(back * vals, axis=0, keepdims=True)
+
+    @pl.loop(0, seqs)
+    def _(s):
+        at = span_of(s, length)
+        b_in, c_out = matrices(s)
+        ds = dscore[s].astype(bf16)
+        b_cols, c_cols = slice(quarter, quarter + STATE), slice(quarter + STATE, active)
+        dz[at, b_cols] = dot(ds, c_out, contract_tokens) * dact[at, b_cols]
+        dz[at, c_cols] = dot(ds, b_in) * dact[at, c_cols]
+
+    back_cum = sharp(x1[...], to_heads)
+    back_step = sharp(x2[...], to_heads)
+    upper = jnp.where(iota((length, length), 0) <= iota((length, length), 1), 1.0, 0.0)
+    back_decay = jnp.concatenate(
+        [sharp(upper, back_cum[s * length : (s + 1) * length]) for s in range(seqs)], axis=0
+    )
+    back_raw = (back_step - back_decay * rate) * sgate[...]
+    bproj[:, active:] = back_raw.astype(bf16)
+    flat[conv_tiles] = jnp.concatenate(
+        [norm_part[:1, n * LANES : (n + 1) * LANES] for n in range(tiles)]
+        + [
+            jnp.sum(back_raw, axis=0, keepdims=True),
+            jnp.sum(back_decay * ldec[...], axis=0, keepdims=True),
+            sharp(skip_part[...], to_heads)[:1],
+            jnp.zeros((8 - tiles - 3, LANES), f32),
+        ],
+        axis=0,
+    )
+
+    @pl.loop(0, conv_tiles)
+    def _(n):
+        cols, where = span_of(n, LANES), span_of(conv_tile(n), LANES)
+        tap = taps[:, where]
+        grads = [jnp.zeros((1, LANES), f32) for _ in range(CONV + 1)]
+        for s in range(seqs):
+            at = slice(s * length, (s + 1) * length)
+            x = proj[at, cols].astype(f32)
+            back = dz[at, cols]
+            dx = back * tap[CONV - 1 : CONV]
+            grads[CONV] += jnp.sum(back, axis=0, keepdims=True)
+            grads[CONV - 1] += jnp.sum(back * x, axis=0, keepdims=True)
+            for k in range(1, CONV):
+                kept = back * mk[s, k - 1]
+                dx = dx + tap[CONV - 1 - k : CONV - k] * pltpu.roll(kept, length - k, 0)
+                grads[CONV - 1 - k] += jnp.sum(kept * pltpu.roll(x, k, 0), axis=0, keepdims=True)
+            bproj[at, cols] = dx.astype(bf16)
+        flat[n] = jnp.concatenate(grads + [jnp.zeros((8 - CONV - 1, LANES), f32)], axis=0)
+
+    for tt in order:
+        got = dot(tall_cols(nall, pl.ds(tt * block, block)), bproj[...], contract_tokens).astype(bf16)
+        gr_conv[tt] = got.reshape(gr_conv.shape[1:])
+        mail.start(
+            lambda tt=tt: gr_conv.at[tt, 1 - m], lambda tt=tt: y_conv.at[tt], lambda tt=tt: ry_conv.at[tt],
+            dev(t, 1 - m, c),
+        )
+
+    def add_blocks(target, left, right):
+        *lead, tall_rows, cols = target.shape
+        piece = 32
+        for at in [()] if not lead else [(i,) for i in range(lead[0])]:
+
+            @pl.loop(0, tall_rows // piece)
+            def _(i, at=at):
+                where = at + (span_of(i, piece),)
+                target[where] = add(left[where], right[where])
+
+    def reduce_line(own, y_got, y_sem, line, low, low_sem, high, high_sem, ok=None):
+        def both(a, b):
+            return b if a is None else a & b
+
+        def pair(tt):
+            def act_():
+                mail.arrive(y_got.at[tt], y_sem.at[tt], here)
+                add_blocks(line.at[tt], own(tt), y_got.at[tt])
+
+            mail.run(act_, ok)
+
+        for tt in order:
+            pair(tt)
+            up = tt >= top // 2
+            for direction in ((1, -1) if up else (-1, 1)):
+                if direction == 1 and tt > 0:
+                    inward = both(ok, (t < tt) & (t > 0))
+
+                    def take(tt=tt):
+                        mail.arrive(low.at[tt], low_sem.at[tt], here)
+                        add_blocks(line.at[tt], line.at[tt], low.at[tt])
+
+                    mail.run(take, inward)
+                    mail.start(
+                        lambda tt=tt: line.at[tt], lambda tt=tt: low.at[tt], lambda tt=tt: low_sem.at[tt],
+                        dev(t + 1, m, c), both(ok, t < tt),
+                    )
+                if direction == -1 and tt < top - 1:
+                    inward = both(ok, (t > tt) & (t < top - 1))
+
+                    def take(tt=tt):
+                        mail.arrive(high.at[tt], high_sem.at[tt], here)
+                        add_blocks(line.at[tt], line.at[tt], high.at[tt])
+
+                    mail.run(take, inward)
+                    mail.start(
+                        lambda tt=tt: line.at[tt], lambda tt=tt: high.at[tt], lambda tt=tt: high_sem.at[tt],
+                        dev(t - 1, m, c), both(ok, t > tt),
+                    )
+
+        def last_low():
+            mail.arrive(low.at[t], low_sem.at[t], here)
+            add_blocks(line.at[t], line.at[t], low.at[t])
+
+        def last_high():
+            mail.arrive(high.at[t], high_sem.at[t], here)
+            add_blocks(line.at[t], line.at[t], high.at[t])
+
+        mail.run(last_low, both(ok, t > 0))
+        mail.run(last_high, both(ok, t < top - 1))
+
+    def hand_over(line, own, receive):
+        own[g, c] = line[t, c]
+        for gg, cc in ((g, 1 - c), (1 - g, c), (1 - g, 1 - c)):
+            mail.start(
+                lambda cc=cc: line.at[t, cc], lambda: own.at[g, c], lambda: receive.at[g, c],
+                dev_g(gg, t, m, cc),
+            )
+
+    def take_over(own, receive):
+        for gg, cc in ((g, 1 - c), (1 - g, c), (1 - g, 1 - c)):
+            mail.arrive(own.at[gg, cc], receive.at[gg, cc], here)
+
+    reduce_line(
+        lambda tt: gr_out.at[tt], y_out, ry_out, line_out, low_out, rl_out, high_out, rh_out, keeper
+    )
+    mail.run(lambda: own_out.__setitem__(Ellipsis, line_out[t]), keeper & holder)
+    mail.start(
+        lambda: line_out.at[t], lambda: own_out, lambda: ro_out.at[0], dev_g(g, t, m, 1 - c),
+        keeper & (c != g),
+    )
+    mail.start(
+        lambda: line_out.at[t], lambda: own_out, lambda: ro_out.at[0], dev_g(1 - g, t, m, g), keeper
+    )
+    reduce_line(
+        lambda tt: gr_gate.at[tt, m], y_gate, ry_gate, line_gate, low_gate, rl_gate, high_gate, rh_gate
+    )
+    hand_over(line_gate, own_gate, ro_gate)
+
+    @pl.loop(0, width // wide_cols)
+    def _(n):
+        at = span_of(n, wide_cols)
+        slots = pl.ds(n * (wide_cols // rows), wide_cols // rows)
+        value = dot(bproj[...], conv_all[slots].reshape(wide_cols, conv_cols), contract_rows)
+        value = value + dot(bgates[...], gate_all[slots].reshape(wide_cols, quarter), contract_rows)
+        part_i[:, :, at] = value.astype(bf16).reshape(4, count, wide_cols)
+        seen = tall_cols(nall, at).astype(f32)
+        pre_part[:, at] = jnp.broadcast_to(
+            jnp.sum(value * seen, axis=0, keepdims=True) / pre_gain[:, at], (8, wide_cols)
+        )
+
+    for slot, device in group:
+        mail.start(
+            lambda slot=slot: part_i.at[slot], lambda: got_i.at[mine], lambda: r_part.at[1, mine], device
+        )
+    flat[conv_tiles + 1] = jnp.concatenate(
+        [pre_part[:1, n * LANES : (n + 1) * LANES] for n in range(width // LANES)], axis=0
+    )
+    mail.start(lambda: flat, lambda: flat_y, lambda: r_flat.at[0, 0], dev(t, 1 - m, c))
+
+    reduce_line(
+        lambda tt: gr_conv.at[tt, m], y_conv, ry_conv, line_conv, low_conv, rl_conv, high_conv, rh_conv
+    )
+    hand_over(line_conv, own_conv, ro_conv)
+
+    mail.arrive(flat_y, r_flat.at[0, 0], here)
+    flat_z[t] = flat[...] + flat_y[...]
+    for d in range(1, top):
+        mail.start(
+            lambda: flat_z.at[t], lambda: flat_z.at[t], lambda: r_flat.at[1, t],
+            dev(lax.rem(t + d, top), m, c),
+        )
+
+    got_b[mine] = part_b[mine]
+    got_i[mine] = part_i[mine]
+    for k in range(2):
+        for slot, _ in group:
+            mail.arrive((got_b, got_i)[k].at[slot], r_part.at[k, slot], here)
+
+    @pl.loop(0, count // 16)
+    def _(i):
+        at = span_of(i, 16)
+        x = tokens[at].astype(f32)
+        branch = sum(got_b[q, at].astype(f32) for q in range(4))
+        back = sum(got_i[q, at].astype(f32) for q in range(4)) * pre_gain[...]
+        block_output[at] = (x + branch).astype(bf16)
+        scale = lax.rsqrt(jnp.mean(x * x, axis=1, keepdims=True) + norm_epsilon)
+        shared = jnp.mean(x * back, axis=1, keepdims=True) * (scale * scale * scale)
+        tokens_grad[at] = cotangent[at].astype(f32) + back * scale - x * shared
+
+    for d in range(1, top):
+        slot = lax.rem(t - d + top, top)
+        mail.arrive(flat_z.at[slot], r_flat.at[1, slot], here)
+    value = flat_z[0]
+    for k in range(1, top):
+        value = value + flat_z[k]
+    flat_all[mine] = value
+    for slot, device in group:
+        mail.start(lambda: flat_all.at[mine], lambda: flat_all.at[mine], lambda: r_flat.at[2, mine], device)
+
+    mail.run(lambda: mail.arrive(own_out, ro_out.at[0], here), jnp.logical_not(holder & keeper))
+    out_grad[...] = own_out[...].astype(f32)
+
+    def put_tiles(base, own, first, number):
+        for gg in range(2):
+            for cc in range(2):
+                for n in range(number):
+                    j = base + 4 * n + 2 * cc + gg
+                    in_grad[:, j * LANES : (j + 1) * LANES] = own[
+                        gg, cc, :, n * LANES : (n + 1) * LANES
+                    ].astype(f32)
+
+    take_over(own_gate, ro_gate)
+    put_tiles(0, own_gate, 0, tiles)
+
+    for slot, _ in group:
+        mail.arrive(flat_all.at[slot], r_flat.at[2, slot], here)
+    parts = [(gg, cc, flat_all.at[2 * cc + gg]) for gg in range(2) for cc in range(2)]
+
+    def selector_of(gg, cc):
+        loc, glob = iota((LANES, LANES), 0), iota((LANES, LANES), 1)
+        wanted = 8 * (loc // 2) + 4 * cc + 2 * gg + loc % 2
+        return jnp.where((glob == wanted) & (loc < local_heads), 1.0, 0.0)
+
+    for gg, cc, part in parts:
+        for n in range(tiles):
+            j = 4 * n + 2 * cc + gg
+            at = slice(j * LANES, (j + 1) * LANES)
+            taps_grad[:, at] = part[n, :CONV]
+            bias_grad[:, at] = part[n, CONV : CONV + 1]
+            norm_grad[:, at] = part[conv_tiles, n : n + 1]
+    for n in range(tiles, conv_tiles):
+        j = n - tiles + inner // LANES
+        at = slice(j * LANES, (j + 1) * LANES)
+        value = sum(part[n] for _, _, part in parts)
+        taps_grad[:, at] = value[:CONV]
+        bias_grad[:, at] = value[CONV : CONV + 1]
+    heads_grad[...] = sum(
+        sharp(part[conv_tiles], selector_of(gg, cc)) for gg, cc, part in parts
+    )
+    value = sum(part[conv_tiles + 1] for _, _, part in parts)
+    for n in range(width // LANES):
+        pre_grad[:, n * LANES : (n + 1) * LANES] = value[n : n + 1]
+
+    take_over(own_conv, ro_conv)
+    put_tiles(inner // LANES, own_conv, 0, tiles)
+    shared = sum(own_conv[gg, cc, :, quarter:active].astype(f32) for gg, cc, _ in parts)
+    in_grad[:, 2 * inner : 2 * inner + states] = shared
+    ends = sum(dot(own_conv[gg, cc, :, active:], selector_of(gg, cc).astype(bf16)) for gg, cc, _ in parts)
+    in_grad[:, 2 * inner + states :] = ends[:, :heads]
+    mail.finish()
+
+
+def params_heads(inner):
+    return inner // HEAD_DIM
+
+
+def fused(
+    tokens, cotangent, documents, in_weight, kernel_taps, kernel_bias, step_bias, decay_log, skip_gain,
+    pre_gain, norm_gain, out_weight,
+):
+    shards = lax.axis_size("fsdp")
+    top, mid = factors(shards)
+    count, width = tokens.shape
+    length = documents.shape[1]
+    total = 2 * length
+    rows, columns = in_weight.shape
+    inner = norm_gain.shape[0]
+    channels = kernel_bias.shape[0]
+    quarter = inner // 4
+    tiles = quarter // LANES
+    conv_tiles = tiles + (channels - inner) // LANES
+    conv_cols = (conv_tiles + 1) * LANES
+    active = conv_tiles * LANES
+    heads = step_bias.shape[0]
+    local_heads = heads // 4
+    own_rows = out_weight.shape[0]
+    params = jnp.pad(jnp.stack([step_bias, decay_log, skip_gain]), ((0, 5), (0, LANES - heads)))
+    vmem = pl.BlockSpec(memory_space=pltpu.VMEM)
+    V = pltpu.VMEM
+    dma = pltpu.SemaphoreType.DMA
+    shape = jax.ShapeDtypeStruct
+    outs = [
+        shape((count, width), bf16), shape((count, width), f32), shape((rows, columns), f32),
+        shape((CONV, channels), f32), shape((1, channels), f32), shape((8, LANES), f32),
+        shape((1, width), f32), shape((1, inner), f32), shape((own_rows, width), f32),
+    ]
+    line_shapes = [(own_rows, width), (2, rows, quarter), (2, rows, conv_cols)]
+    scratch = [
+        V((4, count, width), bf16), V((4, count, width), bf16), V((2, 8, length), f32),
+        V((rows, conv_cols), bf16), V((rows, quarter), bf16),
+        V((shards, rows, conv_cols), bf16), V((shards, rows, quarter), bf16), V((top, own_rows, width), bf16),
+        V((total, conv_cols), bf16), V((total, active), f32), V((total, active), f32),
+        V((2, CONV - 1, length, LANES), f32), V((2, length, length), f32),
+        V((total, LANES), f32), V((total, LANES), f32), V((total, LANES), f32),
+        V((total, LANES), f32), V((2, LANES, length), f32), V((local_heads, total, LANES), f32),
+        V((total, quarter), f32), V((8, quarter), f32), V((total, quarter), bf16),
+        V((2, length, length), f32), V((2 * local_heads, length, length), f32),
+        V((2 * local_heads, length, length), bf16), V((total, quarter), f32), V((total, quarter), bf16),
+        V((total, quarter), bf16), V((total, quarter), f32), V((1, quarter), f32),
+        V((total, LANES), f32), V((4, 8, total), f32), V((total, LANES), f32),
+        V((total, quarter), bf16), V((total, quarter), bf16), V((total, quarter), bf16),
+        V((8, quarter), f32), V((4, count, width), bf16), V((4, count, width), bf16),
+        V((2, length, length), f32), V((total, quarter), f32), V((total, quarter), f32),
+        V((total, active), f32), V((8, quarter), f32), V((total, conv_cols), bf16), V((8, width), f32),
+        V((top, own_rows, width), bf16), V((top, 2, 2, rows, quarter), bf16),
+        V((top, 2, 2, rows, conv_cols), bf16),
+    ]
+    for _ in range(4):
+        scratch += [V((top,) + item, bf16) for item in line_shapes]
+    flat_shape = (conv_tiles + 2, 8, LANES)
+    scratch += [
+        V((own_rows, width), bf16), V((2, 2, rows, quarter), bf16), V((2, 2, rows, conv_cols), bf16),
+        V(flat_shape, f32), V(flat_shape, f32), V((top,) + flat_shape, f32), V((4,) + flat_shape, f32),
+        V((4, count, width), bf16), V((4, count, width), bf16),
+        dma((400,)), dma((2, 4)), dma((1,)), dma((shards,)), dma((shards,)), dma((top,)), dma((4,)),
+        dma((2, 4)),
+    ]
+    scratch += [dma((top,)) for _ in range(9)]
+    scratch += [dma((1,)), dma((2, 2)), dma((2, 2)), dma((3, max(4, top)))]
+    results = pl.pallas_call(
+        functools.partial(fused_kernel, top),
+        out_shape=outs,
+        in_specs=[vmem] * 10,
+        out_specs=[vmem] * len(outs),
+        scratch_shapes=scratch,
+        compiler_params=pltpu.CompilerParams(
+            collective_id=2, has_side_effects=True, vmem_limit_bytes=VMEM_LIMIT
+        ),
+    )(
+        tokens, cotangent, documents, in_weight, kernel_taps, kernel_bias.reshape(1, -1), params,
+        pre_gain.reshape(1, -1), norm_gain.reshape(1, -1), out_weight,
+    )
+    block_output, tokens_grad, in_grad, taps_grad, bias_grad, heads_grad, pre_grad, norm_grad, out_grad = results
+    return (
+        block_output, tokens_grad, in_grad, taps_grad, bias_grad.reshape(-1),
+        heads_grad[4, :heads], heads_grad[5, :heads], heads_grad[6, :heads],
+        pre_grad.reshape(-1), norm_grad.reshape(-1), out_grad,
+    )
+
+
+def fits(tokens, documents, in_weight, norm_gain, out_weight):
+    groups, shards = lax.axis_size("seq"), lax.axis_size("fsdp")
+    top, mid = factors(shards)
+    length, inner = documents.shape[1], norm_gain.shape[0]
+    heads = inner // HEAD_DIM
+    return (
+        groups == 2 and mid == 2 and top % 2 == 0 and length == min(SPAN, length)
+        and tokens.shape[0] * groups == length and length % LANES == 0
+        and out_weight.shape[0] == LANES and inner == shards * LANES
+        and inner // 4 == top * LANES and heads % 32 == 0 and heads <= LANES
+        and in_weight.shape[0] * shards == tokens.shape[1]
+    )
+
+
+def local(*arrays):
+    tokens, _, documents, in_weight = arrays[:4]
+    if fits(tokens, documents, in_weight, arrays[10], arrays[11]):
+        return fused(*arrays)
+    return general(*arrays)
+
+
 def solution(mesh):
     rows = P(("fsdp", "seq"), None)
     split = P("fsdp", None)

time: 234 us -> 166 us (0.71)
  matrix products: 35.8 us -> 0 us
  other arithmetic: 31.2 us -> 2.61 us
  Pallas kernels: 126 us -> 152 us
  local copies, waits for them, and re-layouts: 34.4 us -> 9.8 us
  blocking collectives: 4.11 us -> 0 us
    dot_general x15 -> x0, matrix products: 35.8 us -> none  [the longest x9 24.4 us: dot(): return lax.dot_general(left, right, dims, preferred_element_type=f32)]
    pallas_call x2 -> x1, Pallas kernels: 126 us -> 152 us  [fused(): pl.pallas_call(functools.partial(fused_kernel, top), out_shape=outs, in_s...]
    convert_element_type x3 -> x0, local copies, waits for them, and re-layouts: 7.67 us -> none  [the longest x1 3.12 us: local(): conv_grad = dot(normed_in, back_projected, contract_tokens).astype(bf16)]
    reduce_sum x9 -> x0, other arithmetic: 7.29 us -> none  [the longest x2 2.07 us: mixer(): summed = summed + taps[CONV - 1 - offset] * shifted * matched[:, None]]
    slice x27 -> x0, local copies, waits for them, and re-layouts: 7.27 us -> none  [the longest x5 2.53 us: local(): totals.append(flat[start:start + piece.size].reshape(piece.shape))]
    reshape x38 -> x1, local copies, waits for them, and re-layouts: 8.36 us -> 1.31 us  [fused(): kernel_bias.reshape(1, -1)]
    another operation x7 -> x1, other arithmetic: 7.92 us -> 1.29 us  [fused(): jnp.stack([step_bias, decay_log, skip_gain])]
    convert_element_type x4 -> x0, other arithmetic: 5.07 us -> none  [the longest x1 2.86 us: local(): back_mixed = (back_gated * silu).astype(bf16).astype(f32)]
where the time goes in v1:
time: 166 us; the launch traced here: 165 us
  Pallas kernels  152 us (92%)
  local copies, waits for them, and re-layouts  9.8 us (6%)
  other arithmetic  2.61 us (2%)
    pallas_call x1, Pallas kernels, fused(): pl.pallas_call(functools.partial(fused_kernel, top), out_shape=outs, in_s...  152 us
    unnamed x17, local copies, waits for them, and re-layouts  7.18 us

profile of v1, /device:TPU:1, one launch (start us, length us, event | category | flops | bytes accessed | tf_op | source)
XLA Modules:
  0.0 165.4 jit_solution(17501985821903172882)
XLA Ops:
  0.6 1.3 reshape.40.refs_5_
  2.0 1.3 select_maximum_fusion.refs_6_
  3.2 152.3 %shard_map.203 = (bf16[128,1024]{1,0:T(8,128)(2,1)}, f32[128,1024]{1,0:T(8,128)}, f32[64,4384]{1,0:T(8,128)}, f32[4,2304]{1,0:T(4,128)}, f32[1,2304]{1,0:T(1,128...) custom-call(bf16[128,1024]{1,0:T(8,128)(2,1)} %refs_0_.1, ...), custom_call_target="tpu_custom_call" | custom-call | tf_op jit(solution)/shard_map/pallas_call | solution.py:1369
  155.6 0.0 copy-start
  155.6 1.3 slice_bitcast_fusion
  156.9 1.3 reduce
  158.2 1.7 %copy.30 = bf16[128,1024]{1,0:T(8,128)(2,1)} copy(bf16[128,1024]{1,0:T(8,128)(2,1)} %get-tuple-element.43) | data formatting | bytes 524288
  159.9 1.9 %copy.31 = f32[128,1024]{1,0:T(8,128)} copy(f32[128,1024]{1,0:T(8,128)} %get-tuple-element.44) | data formatting | bytes 1048576
  161.8 0.0 copy-done
  161.8 0.0 copy-start.2
  161.8 0.0 copy-start.4
  161.8 0.0 copy-start.3
  161.8 0.0 copy-start.1
  161.8 1.0 copy.32
  162.8 0.0 copy-done.2
  162.8 0.6 copy.33
  163.4 0.0 copy-done.4
  163.4 0.6 copy.34
  164.0 0.0 copy-done.3
  164.0 0.6 copy.35
  164.6 0.0 copy-done.1
  164.6 0.8 copy.36
Async XLA Ops:
  155.6 6.2 %copy-start = (f32[64,4384]{1,0:T(8,128)S(1)}, f32[64,4384]{1,0:T(8,128)}, u32[]{:S(2)}) copy-start(f32[64,4384]{1,0:T(8,128)} %get-tuple-element.45) | copy-start | bytes 3366916
  161.8 1.0 copy-start.2
  161.8 1.6 copy-start.4
  161.8 2.2 %copy-start.3 = (f32[1,2048]{1,0:T(1,128)S(1)}, f32[1,2048]{1,0:T(1,128)}, u32[]{:S(2)}) copy-start(f32[1,2048]{1,0:T(1,128)} %get-tuple-element.27) | copy-start | bytes 24580
  161.8 2.8 %copy-start.1 = (f32[128,1024]{1,0:T(8,128)S(1)}, f32[128,1024]{1,0:T(8,128)}, u32[]{:S(2)}) copy-start(f32[128,1024]{1,0:T(8,128)} %get-tuple-element.53) | copy-start | bytes 1572868

commit v2 on v1

--- a/solution.py
+++ b/solution.py
@@ -589,6 +589,7 @@
 
 LANES = 128
 FAR = -1e30
+SENDS = 130
 exact = lax.Precision.HIGHEST
 
 
@@ -609,6 +610,7 @@
         self.send = send
         self.count = 0
         self.made = []
+        self.stays = []
 
     def start(self, source, target, receive, device, when=None):
         slot = self.count
@@ -643,25 +645,32 @@
             device_id_type=MESH,
         ).wait_recv()
 
+    def local(self, source, target, sem, when=None):
+        make = lambda: pltpu.make_async_copy(source(), target(), sem)
+        self.stays.append((make, when))
+        self.run(lambda: make().start(), when)
+
     def finish(self):
+        for make, when in self.stays:
+            self.run(lambda make=make: make().wait(), when)
         for make, when in self.made:
             self.run(lambda make=make: make().wait_send(), when)
 
 
 def fused_kernel(top, *refs):
     (
-        tokens, cotangent, documents, in_weight, taps, tap_bias, params, pre_gain, norm_gain, out_weight,
-        block_output, tokens_grad, in_grad, taps_grad, bias_grad, heads_grad, pre_grad, norm_grad, out_grad,
+        tokens, cotangent, documents, in_weight, taps, params, pre_gain, norm_gain, out_weight,
+        got_b, got_i, own_out, own_gate, own_conv, flat_all,
         nall, call, docs, conv_pack, gate_pack, conv_all, gate_all, out_all,
         proj, act, dact, mk, bias_mask, step, ldec, sgate, cum, cum_t, cum_b, step_e, skip_e, scaled,
         scores, decay, weigh, inside, mixed, gates, bnorm, gain_own, sums, sums_all, totals,
         normed_bf, bmixed, bgates, norm_part, part_b, part_i, dscore, x1, x2, dz, skip_part, bproj, pre_part,
         gr_out, gr_gate, gr_conv, y_out, y_gate, y_conv, line_out, line_gate, line_conv,
         low_out, low_gate, low_conv, high_out, high_gate, high_conv,
-        own_out, own_gate, own_conv, flat, flat_y, flat_z, flat_all, got_b, got_i,
+        flat, flat_y, flat_z, flat_own,
         send, r_rows, r_docs, r_conv, r_gate, r_out, r_sums, r_part,
         ry_out, ry_gate, ry_conv, rl_out, rl_gate, rl_conv, rh_out, rh_gate, rh_conv,
-        ro_out, ro_gate, ro_conv, r_flat,
+        ro_out, ro_gate, ro_conv, r_flat, r_local,
     ) = refs
     mid = 2
     me, t, m, c = position(top, mid)
@@ -729,6 +738,10 @@
     pack(conv_pack, None, 1 - c)
     pl.semaphore_wait(barrier, len(greeted))
 
+    near = t + 1 - 2 * lax.rem(t, 2)
+    far = lax.rem(t + top // 2, top)
+    last = lax.rem(near + top // 2, top)
+
     def spread(mine_ref, pack_ref, all_ref, receive):
         for src, cc in ((mine_ref, c), (lambda: pack_ref, 1 - c)):
             for up in (1, -1):
@@ -851,7 +864,7 @@
     relay(gate_all, r_gate, 1)
     relay_rows(1)
 
-    chosen = sharp(params[...], selector(c))
+    chosen = sharp(params[:8], selector(c))
     rate = jnp.exp(chosen[1:2])
     raw = proj[:, active:].astype(f32) + chosen[:1]
     step[...] = jnp.maximum(raw, 0.0) + jnp.log1p(jnp.exp(-jnp.abs(raw)))
@@ -879,7 +892,7 @@
         where = span_of(conv_tile(n), LANES)
         x = proj[at, cols].astype(f32)
         tap = taps[:, where]
-        z = tap_bias[:, where] + x * tap[CONV - 1 : CONV]
+        z = params[pl.ds(8 + conv_tile(n), 1)] + x * tap[CONV - 1 : CONV]
         for k in range(1, CONV):
             z = z + tap[CONV - 1 - k : CONV - k] * (pltpu.roll(x, k, 0) * mk[s, k - 1])
         sig = jax.nn.sigmoid(z)
@@ -985,25 +998,77 @@
     def tall_cols(ref, at):
         return ref[:, :, at].reshape(total, at.size)
 
-    order = []
-    for k in range(top // 2):
-        order += [top - 1 - k, k]
-
-    for tt in order:
-        cols = slice(tt * LANES, (tt + 1) * LANES)
-        gr_out[tt] = dot(normed_bf[:, cols], tall(call), contract_tokens).astype(bf16)
+    def add_blocks(target, left, right):
+        *lead, tall_rows, cols = target.shape
+        piece = 32
+        for at in [()] if not lead else [(i,) for i in range(lead[0])]:
+
+            @pl.loop(0, tall_rows // piece)
+            def _(i, at=at):
+                where = at + (span_of(i, piece),)
+                target[where] = add(left[where], right[where])
+
+    def reducer(own, y_got, y_sem, line, low, low_sem, high, high_sem, ok=None):
+        def step(r):
+            def take():
+                mail.arrive(y_got.at[r], y_sem.at[r], here)
+                add_blocks(line.at[r], own(r), y_got.at[r])
+                if r >= 2:
+                    mail.arrive(low.at[r - 2], low_sem.at[r - 2], here)
+                    add_blocks(line.at[r], line.at[r], low.at[r - 2])
+                if r == 3:
+                    mail.arrive(high.at[0], high_sem.at[0], here)
+                    add_blocks(line.at[r], line.at[r], high.at[0])
+
+            mail.run(take, ok)
+            if r < 2:
+                mail.start(
+                    lambda: line.at[r], lambda: low.at[r], lambda: low_sem.at[r], dev(near, m, c), ok
+                )
+            if r == 2:
+                mail.start(
+                    lambda: line.at[r], lambda: high.at[0], lambda: high_sem.at[0], dev(far, m, c), ok
+                )
+
+        return step
+
+    def hand_over(line, own, receive, at):
+        mail.local(lambda: line.at[3, c], lambda: own.at[g, c], r_local.at[at])
+        for gg, cc in ((g, 1 - c), (1 - g, c), (1 - g, 1 - c)):
+            mail.start(
+                lambda cc=cc: line.at[3, cc], lambda: own.at[g, c], lambda: receive.at[g, c],
+                dev_g(gg, t, m, cc),
+            )
+
+    def take_over(own, receive):
+        for gg, cc in ((g, 1 - c), (1 - g, c), (1 - g, 1 - c)):
+            mail.arrive(own.at[gg, cc], receive.at[gg, cc], here)
+
+    out_step = reducer(
+        lambda r: gr_out.at[r], y_out, ry_out, line_out, low_out, rl_out, high_out, rh_out, keeper
+    )
+    gate_step = reducer(
+        lambda r: gr_gate.at[r, m], y_gate, ry_gate, line_gate, low_gate, rl_gate, high_gate, rh_gate
+    )
+    conv_step = reducer(
+        lambda r: gr_conv.at[r, m], y_conv, ry_conv, line_conv, low_conv, rl_conv, high_conv, rh_conv
+    )
+    order = (last, near, far, t)
+    block = width // top
+
+    for r in range(top):
+        got = dot(tall_cols(nall, span_of(order[r], block)), bgates[...], contract_tokens).astype(bf16)
+        gr_gate[r] = got.reshape(gr_gate.shape[1:])
         mail.start(
-            lambda tt=tt: gr_out.at[tt], lambda tt=tt: y_out.at[tt], lambda tt=tt: ry_out.at[tt],
+            lambda r=r: gr_gate.at[r, 1 - m], lambda r=r: y_gate.at[r], lambda r=r: ry_gate.at[r],
+            dev(t, 1 - m, c),
+        )
+
+    for r in range(top):
+        gr_out[r] = dot(normed_bf[:, span_of(order[r], LANES)], tall(call), contract_tokens).astype(bf16)
+        mail.start(
+            lambda r=r: gr_out.at[r], lambda r=r: y_out.at[r], lambda r=r: ry_out.at[r],
             dev(t, 1 - m, c), c != m,
-        )
-
-    block = width // top
-    for tt in order:
-        got = dot(tall_cols(nall, pl.ds(tt * block, block)), bgates[...], contract_tokens).astype(bf16)
-        gr_gate[tt] = got.reshape(gr_gate.shape[1:])
-        mail.start(
-            lambda tt=tt: gr_gate.at[tt, 1 - m], lambda tt=tt: y_gate.at[tt], lambda tt=tt: ry_gate.at[tt],
-            dev(t, 1 - m, c),
         )
 
     @pl.loop(0, width // wide_cols)
@@ -1016,6 +1081,7 @@
         mail.start(
             lambda slot=slot: part_b.at[slot], lambda: got_b.at[mine], lambda: r_part.at[0, mine], device
         )
+    mail.local(lambda: part_b.at[mine], lambda: got_b.at[mine], r_local.at[3])
 
     skip_part[...] = jnp.zeros_like(skip_part)
     dscore[...] = jnp.zeros_like(dscore)
@@ -1041,6 +1107,7 @@
         dz[at, cols] = (back * skip_e[2:3, cols] + ds * step_e[at, cols]) * dact[at, cols]
         skip_part[:, cols] += jnp.sum(back * vals, axis=0, keepdims=True)
 
+    gate_step(0)
     @pl.loop(0, seqs)
     def _(s):
         at = span_of(s, length)
@@ -1069,6 +1136,7 @@
         axis=0,
     )
 
+    gate_step(1)
     @pl.loop(0, conv_tiles)
     def _(n):
         cols, where = span_of(n, LANES), span_of(conv_tile(n), LANES)
@@ -1088,103 +1156,16 @@
             bproj[at, cols] = dx.astype(bf16)
         flat[n] = jnp.concatenate(grads + [jnp.zeros((8 - CONV - 1, LANES), f32)], axis=0)
 
-    for tt in order:
-        got = dot(tall_cols(nall, pl.ds(tt * block, block)), bproj[...], contract_tokens).astype(bf16)
-        gr_conv[tt] = got.reshape(gr_conv.shape[1:])
+    for r in range(top):
+        got = dot(tall_cols(nall, span_of(order[r], block)), bproj[...], contract_tokens).astype(bf16)
+        gr_conv[r] = got.reshape(gr_conv.shape[1:])
         mail.start(
-            lambda tt=tt: gr_conv.at[tt, 1 - m], lambda tt=tt: y_conv.at[tt], lambda tt=tt: ry_conv.at[tt],
+            lambda r=r: gr_conv.at[r, 1 - m], lambda r=r: y_conv.at[r], lambda r=r: ry_conv.at[r],
             dev(t, 1 - m, c),
         )
 
-    def add_blocks(target, left, right):
-        *lead, tall_rows, cols = target.shape
-        piece = 32
-        for at in [()] if not lead else [(i,) for i in range(lead[0])]:
-
-            @pl.loop(0, tall_rows // piece)
-            def _(i, at=at):
-                where = at + (span_of(i, piece),)
-                target[where] = add(left[where], right[where])
-
-    def reduce_line(own, y_got, y_sem, line, low, low_sem, high, high_sem, ok=None):
-        def both(a, b):
-            return b if a is None else a & b
-
-        def pair(tt):
-            def act_():
-                mail.arrive(y_got.at[tt], y_sem.at[tt], here)
-                add_blocks(line.at[tt], own(tt), y_got.at[tt])
-
-            mail.run(act_, ok)
-
-        for tt in order:
-            pair(tt)
-            up = tt >= top // 2
-            for direction in ((1, -1) if up else (-1, 1)):
-                if direction == 1 and tt > 0:
-                    inward = both(ok, (t < tt) & (t > 0))
-
-                    def take(tt=tt):
-                        mail.arrive(low.at[tt], low_sem.at[tt], here)
-                        add_blocks(line.at[tt], line.at[tt], low.at[tt])
-
-                    mail.run(take, inward)
-                    mail.start(
-                        lambda tt=tt: line.at[tt], lambda tt=tt: low.at[tt], lambda tt=tt: low_sem.at[tt],
-                        dev(t + 1, m, c), both(ok, t < tt),
-                    )
-                if direction == -1 and tt < top - 1:
-                    inward = both(ok, (t > tt) & (t < top - 1))
-
-                    def take(tt=tt):
-                        mail.arrive(high.at[tt], high_sem.at[tt], here)
-                        add_blocks(line.at[tt], line.at[tt], high.at[tt])
-
-                    mail.run(take, inward)
-                    mail.start(
-                        lambda tt=tt: line.at[tt], lambda tt=tt: high.at[tt], lambda tt=tt: high_sem.at[tt],
-                        dev(t - 1, m, c), both(ok, t > tt),
-                    )
-
-        def last_low():
-            mail.arrive(low.at[t], low_sem.at[t], here)
-            add_blocks(line.at[t], line.at[t], low.at[t])
-
-        def last_high():
-            mail.arrive(high.at[t], high_sem.at[t], here)
-            add_blocks(line.at[t], line.at[t], high.at[t])
-
-        mail.run(last_low, both(ok, t > 0))
-        mail.run(last_high, both(ok, t < top - 1))
-
-    def hand_over(line, own, receive):
-        own[g, c] = line[t, c]
-        for gg, cc in ((g, 1 - c), (1 - g, c), (1 - g, 1 - c)):
-            mail.start(
-                lambda cc=cc: line.at[t, cc], lambda: own.at[g, c], lambda: receive.at[g, c],
-                dev_g(gg, t, m, cc),
-            )
-
-    def take_over(own, receive):
-        for gg, cc in ((g, 1 - c), (1 - g, c), (1 - g, 1 - c)):
-            mail.arrive(own.at[gg, cc], receive.at[gg, cc], here)
-
-    reduce_line(
-        lambda tt: gr_out.at[tt], y_out, ry_out, line_out, low_out, rl_out, high_out, rh_out, keeper
-    )
-    mail.run(lambda: own_out.__setitem__(Ellipsis, line_out[t]), keeper & holder)
-    mail.start(
-        lambda: line_out.at[t], lambda: own_out, lambda: ro_out.at[0], dev_g(g, t, m, 1 - c),
-        keeper & (c != g),
-    )
-    mail.start(
-        lambda: line_out.at[t], lambda: own_out, lambda: ro_out.at[0], dev_g(1 - g, t, m, g), keeper
-    )
-    reduce_line(
-        lambda tt: gr_gate.at[tt, m], y_gate, ry_gate, line_gate, low_gate, rl_gate, high_gate, rh_gate
-    )
-    hand_over(line_gate, own_gate, ro_gate)
-
+    gate_step(2)
+    out_step(0)
     @pl.loop(0, width // wide_cols)
     def _(n):
         at = span_of(n, wide_cols)
@@ -1201,15 +1182,30 @@
         mail.start(
             lambda slot=slot: part_i.at[slot], lambda: got_i.at[mine], lambda: r_part.at[1, mine], device
         )
+    mail.local(lambda: part_i.at[mine], lambda: got_i.at[mine], r_local.at[4])
     flat[conv_tiles + 1] = jnp.concatenate(
         [pre_part[:1, n * LANES : (n + 1) * LANES] for n in range(width // LANES)], axis=0
     )
     mail.start(lambda: flat, lambda: flat_y, lambda: r_flat.at[0, 0], dev(t, 1 - m, c))
 
-    reduce_line(
-        lambda tt: gr_conv.at[tt, m], y_conv, ry_conv, line_conv, low_conv, rl_conv, high_conv, rh_conv
-    )
-    hand_over(line_conv, own_conv, ro_conv)
+    gate_step(3)
+    hand_over(line_gate, own_gate, ro_gate, 0)
+    out_step(1)
+    out_step(2)
+    conv_step(0)
+    conv_step(1)
+    out_step(3)
+    mail.local(lambda: line_out.at[3], lambda: own_out, r_local.at[2], keeper & holder)
+    mail.start(
+        lambda: line_out.at[3], lambda: own_out, lambda: ro_out.at[0], dev_g(g, t, m, 1 - c),
+        keeper & (c != g),
+    )
+    mail.start(
+        lambda: line_out.at[3], lambda: own_out, lambda: ro_out.at[0], dev_g(1 - g, t, m, g), keeper
+    )
+    conv_step(2)
+    conv_step(3)
+    hand_over(line_conv, own_conv, ro_conv, 1)
 
     mail.arrive(flat_y, r_flat.at[0, 0], here)
     flat_z[t] = flat[...] + flat_y[...]
@@ -1219,11 +1215,95 @@
             dev(lax.rem(t + d, top), m, c),
         )
 
-    got_b[mine] = part_b[mine]
-    got_i[mine] = part_i[mine]
+    for d in range(1, top):
+        slot = lax.rem(t - d + top, top)
+        mail.arrive(flat_z.at[slot], r_flat.at[1, slot], here)
+    value = flat_z[0]
+    for k in range(1, top):
+        value = value + flat_z[k]
+    flat_own[...] = value
+    for slot, device in group:
+        mail.start(lambda: flat_own, lambda: flat_all.at[mine], lambda: r_flat.at[2, mine], device)
+    mail.local(lambda: flat_own, lambda: flat_all.at[mine], r_local.at[5])
     for k in range(2):
         for slot, _ in group:
             mail.arrive((got_b, got_i)[k].at[slot], r_part.at[k, slot], here)
+    mail.run(lambda: mail.arrive(own_out, ro_out.at[0], here), jnp.logical_not(holder & keeper))
+    take_over(own_gate, ro_gate)
+    for slot, _ in group:
+        mail.arrive(flat_all.at[slot], r_flat.at[2, slot], here)
+    take_over(own_conv, ro_conv)
+    mail.finish()
+
+
+def finish_kernel(inner, heads, *refs):
+    (
+        tokens, cotangent, pre_gain, got_b, got_i, own_out, own_gate, own_conv, flat_all,
+        *targets,
+    ) = refs
+    outs, scratch, sems = targets[:11], targets[11:22], targets[22]
+    (
+        block_output, tokens_grad, in_grad, taps_grad, bias_grad, step_grad, decay_grad, skip_grad,
+        pre_grad, norm_grad, out_grad,
+    ) = scratch
+    count, width = tokens.shape
+    quarter = inner // 4
+    tiles = quarter // LANES
+    states = taps_grad.shape[1] - inner
+    conv_tiles = tiles + states // LANES
+    active = conv_tiles * LANES
+    local_heads = heads // 4
+
+    def send(*which):
+        for k in which:
+            pltpu.make_async_copy(scratch[k], outs[k], sems.at[k]).start()
+
+    parts = [(gg, cc, flat_all.at[2 * cc + gg]) for gg in range(2) for cc in range(2)]
+
+    def selector_of(gg, cc):
+        loc, glob = iota((LANES, LANES), 0), iota((LANES, LANES), 1)
+        wanted = 8 * (loc // 2) + 4 * cc + 2 * gg + loc % 2
+        return jnp.where((glob == wanted) & (loc < local_heads), 1.0, 0.0)
+
+    def put_tiles(base, own):
+        for gg in range(2):
+            for cc in range(2):
+                for n in range(tiles):
+                    j = base + 4 * n + 2 * cc + gg
+                    in_grad[:, j * LANES : (j + 1) * LANES] = own[
+                        gg, cc, :, n * LANES : (n + 1) * LANES
+                    ].astype(f32)
+
+    put_tiles(0, own_gate)
+    put_tiles(inner // LANES, own_conv)
+    shared = sum(own_conv[gg, cc, :, quarter:active].astype(f32) for gg, cc, _ in parts)
+    in_grad[:, 2 * inner : 2 * inner + states] = shared
+    ends = sum(dot(own_conv[gg, cc, :, active:], selector_of(gg, cc).astype(bf16)) for gg, cc, _ in parts)
+    in_grad[:, 2 * inner + states :] = ends[:, :heads]
+    send(2)
+    out_grad[...] = own_out[...].astype(f32)
+    send(10)
+
+    for gg, cc, part in parts:
+        for n in range(tiles):
+            j = 4 * n + 2 * cc + gg
+            at = slice(j * LANES, (j + 1) * LANES)
+            taps_grad[:, at] = part[n, :CONV]
+            bias_grad[j : j + 1] = part[n, CONV : CONV + 1]
+            norm_grad[:, at] = part[conv_tiles, n : n + 1]
+    for n in range(tiles, conv_tiles):
+        j = n - tiles + inner // LANES
+        value = sum(part[n] for _, _, part in parts)
+        taps_grad[:, j * LANES : (j + 1) * LANES] = value[:CONV]
+        bias_grad[j : j + 1] = value[CONV : CONV + 1]
+    by_head = sum(sharp(part[conv_tiles], selector_of(gg, cc)) for gg, cc, part in parts)
+    step_grad[...] = by_head[tiles : tiles + 1, :heads]
+    decay_grad[...] = by_head[tiles + 1 : tiles + 2, :heads]
+    skip_grad[...] = by_head[tiles + 2 : tiles + 3, :heads]
+    value = sum(part[conv_tiles + 1] for _, _, part in parts)
+    for n in range(width // LANES):
+        pre_grad[:, n * LANES : (n + 1) * LANES] = value[n : n + 1]
+    send(3, 4, 5, 6, 7, 8, 9)
 
     @pl.loop(0, count // 16)
     def _(i):
@@ -1236,67 +1316,9 @@
         shared = jnp.mean(x * back, axis=1, keepdims=True) * (scale * scale * scale)
         tokens_grad[at] = cotangent[at].astype(f32) + back * scale - x * shared
 
-    for d in range(1, top):
-        slot = lax.rem(t - d + top, top)
-        mail.arrive(flat_z.at[slot], r_flat.at[1, slot], here)
-    value = flat_z[0]
-    for k in range(1, top):
-        value = value + flat_z[k]
-    flat_all[mine] = value
-    for slot, device in group:
-        mail.start(lambda: flat_all.at[mine], lambda: flat_all.at[mine], lambda: r_flat.at[2, mine], device)
-
-    mail.run(lambda: mail.arrive(own_out, ro_out.at[0], here), jnp.logical_not(holder & keeper))
-    out_grad[...] = own_out[...].astype(f32)
-
-    def put_tiles(base, own, first, number):
-        for gg in range(2):
-            for cc in range(2):
-                for n in range(number):
-                    j = base + 4 * n + 2 * cc + gg
-                    in_grad[:, j * LANES : (j + 1) * LANES] = own[
-                        gg, cc, :, n * LANES : (n + 1) * LANES
-                    ].astype(f32)
-
-    take_over(own_gate, ro_gate)
-    put_tiles(0, own_gate, 0, tiles)
-
-    for slot, _ in group:
-        mail.arrive(flat_all.at[slot], r_flat.at[2, slot], here)
-    parts = [(gg, cc, flat_all.at[2 * cc + gg]) for gg in range(2) for cc in range(2)]
-
-    def selector_of(gg, cc):
-        loc, glob = iota((LANES, LANES), 0), iota((LANES, LANES), 1)
-        wanted = 8 * (loc // 2) + 4 * cc + 2 * gg + loc % 2
-        return jnp.where((glob == wanted) & (loc < local_heads), 1.0, 0.0)
-
-    for gg, cc, part in parts:
-        for n in range(tiles):
-            j = 4 * n + 2 * cc + gg
-            at = slice(j * LANES, (j + 1) * LANES)
-            taps_grad[:, at] = part[n, :CONV]
-            bias_grad[:, at] = part[n, CONV : CONV + 1]
-            norm_grad[:, at] = part[conv_tiles, n : n + 1]
-    for n in range(tiles, conv_tiles):
-        j = n - tiles + inner // LANES
-        at = slice(j * LANES, (j + 1) * LANES)
-        value = sum(part[n] for _, _, part in parts)
-        taps_grad[:, at] = value[:CONV]
-        bias_grad[:, at] = value[CONV : CONV + 1]
-    heads_grad[...] = sum(
-        sharp(part[conv_tiles], selector_of(gg, cc)) for gg, cc, part in parts
-    )
-    value = sum(part[conv_tiles + 1] for _, _, part in parts)
-    for n in range(width // LANES):
-        pre_grad[:, n * LANES : (n + 1) * LANES] = value[n : n + 1]
-
-    take_over(own_conv, ro_conv)
-    put_tiles(inner // LANES, own_conv, 0, tiles)
-    shared = sum(own_conv[gg, cc, :, quarter:active].astype(f32) for gg, cc, _ in parts)
-    in_grad[:, 2 * inner : 2 * inner + states] = shared
-    ends = sum(dot(own_conv[gg, cc, :, active:], selector_of(gg, cc).astype(bf16)) for gg, cc, _ in parts)
-    in_grad[:, 2 * inner + states :] = ends[:, :heads]
-    mail.finish()
+    send(0, 1)
+    for k in range(len(outs)):
+        pltpu.make_async_copy(scratch[k], outs[k], sems.at[k]).wait()
 
 
 def params_heads(inner):
@@ -1323,15 +1345,21 @@
     heads = step_bias.shape[0]
     local_heads = heads // 4
     own_rows = out_weight.shape[0]
-    params = jnp.pad(jnp.stack([step_bias, decay_log, skip_gain]), ((0, 5), (0, LANES - heads)))
+    params = jnp.concatenate(
+        [
+            jnp.pad(jnp.stack([step_bias, decay_log, skip_gain]), ((0, 5), (0, LANES - heads))),
+            kernel_bias.reshape(-1, LANES),
+        ]
+    )
     vmem = pl.BlockSpec(memory_space=pltpu.VMEM)
     V = pltpu.VMEM
     dma = pltpu.SemaphoreType.DMA
     shape = jax.ShapeDtypeStruct
+    flat_shape = (conv_tiles + 2, 8, LANES)
     outs = [
-        shape((count, width), bf16), shape((count, width), f32), shape((rows, columns), f32),
-        shape((CONV, channels), f32), shape((1, channels), f32), shape((8, LANES), f32),
-        shape((1, width), f32), shape((1, inner), f32), shape((own_rows, width), f32),
+        shape((4, count, width), bf16), shape((4, count, width), bf16), shape((own_rows, width), bf16),
+        shape((2, 2, rows, quarter), bf16), shape((2, 2, rows, conv_cols), bf16),
+        shape((4,) + flat_shape, f32),
     ]
     line_shapes = [(own_rows, width), (2, rows, quarter), (2, rows, conv_cols)]
     scratch = [
@@ -1356,34 +1384,43 @@
     ]
     for _ in range(4):
         scratch += [V((top,) + item, bf16) for item in line_shapes]
-    flat_shape = (conv_tiles + 2, 8, LANES)
+    scratch += [V(flat_shape, f32), V(flat_shape, f32), V((top,) + flat_shape, f32), V(flat_shape, f32)]
     scratch += [
-        V((own_rows, width), bf16), V((2, 2, rows, quarter), bf16), V((2, 2, rows, conv_cols), bf16),
-        V(flat_shape, f32), V(flat_shape, f32), V((top,) + flat_shape, f32), V((4,) + flat_shape, f32),
-        V((4, count, width), bf16), V((4, count, width), bf16),
-        dma((400,)), dma((2, 4)), dma((1,)), dma((shards,)), dma((shards,)), dma((top,)), dma((4,)),
+        dma((SENDS,)), dma((2, 4)), dma((1,)), dma((shards,)), dma((shards,)), dma((top,)), dma((4,)),
         dma((2, 4)),
     ]
     scratch += [dma((top,)) for _ in range(9)]
-    scratch += [dma((1,)), dma((2, 2)), dma((2, 2)), dma((3, max(4, top)))]
+    scratch += [dma((1,)), dma((2, 2)), dma((2, 2)), dma((3, max(4, top))), dma((6,))]
+    hbm = pl.BlockSpec(memory_space=pl.ANY)
     results = pl.pallas_call(
         functools.partial(fused_kernel, top),
         out_shape=outs,
-        in_specs=[vmem] * 10,
-        out_specs=[vmem] * len(outs),
+        in_specs=[vmem] * 9,
+        out_specs=[hbm] * len(outs),
         scratch_shapes=scratch,
         compiler_params=pltpu.CompilerParams(
             collective_id=2, has_side_effects=True, vmem_limit_bytes=VMEM_LIMIT
         ),
     )(
-        tokens, cotangent, documents, in_weight, kernel_taps, kernel_bias.reshape(1, -1), params,
+        tokens, cotangent, documents, in_weight, kernel_taps, params,
         pre_gain.reshape(1, -1), norm_gain.reshape(1, -1), out_weight,
     )
-    block_output, tokens_grad, in_grad, taps_grad, bias_grad, heads_grad, pre_grad, norm_grad, out_grad = results
-    return (
-        block_output, tokens_grad, in_grad, taps_grad, bias_grad.reshape(-1),
-        heads_grad[4, :heads], heads_grad[5, :heads], heads_grad[6, :heads],
-        pre_grad.reshape(-1), norm_grad.reshape(-1), out_grad,
+    outs = [
+        shape((count, width), bf16), shape((count, width), f32), shape((rows, columns), f32),
+        shape((CONV, channels), f32), shape((channels // LANES, LANES), f32), shape((1, heads), f32),
+        shape((1, heads), f32), shape((1, heads), f32), shape((1, width), f32), shape((1, inner), f32),
+        shape((own_rows, width), f32),
+    ]
+    final = pl.pallas_call(
+        functools.partial(finish_kernel, inner, heads),
+        out_shape=outs,
+        in_specs=[vmem] * 9,
+        out_specs=[hbm] * len(outs),
+        scratch_shapes=[V(out.shape, out.dtype) for out in outs] + [dma((len(outs),))],
+        compiler_params=pltpu.CompilerParams(vmem_limit_bytes=VMEM_LIMIT),
+    )(tokens, cotangent, pre_gain.reshape(1, -1), *results)
+    return tuple(
+        out.reshape(-1) if k in (4, 5, 6, 7, 8, 9) else out for k, out in enumerate(final)
     )
 
 
@@ -1393,7 +1430,7 @@
     length, inner = documents.shape[1], norm_gain.shape[0]
     heads = inner // HEAD_DIM
     return (
-        groups == 2 and mid == 2 and top % 2 == 0 and length == min(SPAN, length)
+        groups == 2 and mid == 2 and top == 4 and length == min(SPAN, length)
         and tokens.shape[0] * groups == length and length % LANES == 0
         and out_weight.shape[0] == LANES and inner == shards * LANES
         and inner // 4 == top * LANES and heads % 32 == 0 and heads <= LANES

time: 166 us -> 129 us (0.78)
  Pallas kernels: 152 us -> 126 us
  local copies, waits for them, and re-layouts: 9.8 us -> 0 us
    pallas_call x1, Pallas kernels: 152 us -> 122 us  [fused(): pl.pallas_call(functools.partial(fused_kernel, top), out_shape=outs, in_s...]
    unnamed x17 -> x0, local copies, waits for them, and re-layouts: 7.18 us -> none
    pallas_call x0 -> x1, Pallas kernels: none -> 4.13 us  [fused(): pl.pallas_call(functools.partial(finish_kernel, inner, heads), out_shape=...]
where the time goes in v2:
time: 129 us
  Pallas kernels  126 us (98%)
  other arithmetic  2.02 us (2%)
    pallas_call x1, Pallas kernels, fused(): pl.pallas_call(functools.partial(fused_kernel, top), out_shape=outs, in_s...  122 us
    pallas_call x1, Pallas kernels, fused(): pl.pallas_call(functools.partial(finish_kernel, inner, heads), out_shape=...  4.13 us

profile of v2, /device:TPU:1, one launch (start us, length us, event | category | flops | bytes accessed | tf_op | source)
XLA Modules:
  0.0 128.9 jit_solution(15101551007637132625)
XLA Ops:
  0.6 0.7 select_maximum_fusion
  1.3 1.3 %pad_maximum_fusion.refs_5_ = f32[26,128]{1,0:T(8,128)} fusion(f32[18,128]{1,0:T(8,128)} %bitcast.14, f32[8,128]{1,0:T(8,128)S(1)} %select_maximum_fusion), kind=kLoop, calls=%fused_computation | loop fusion | flops 3328 | bytes 26624 | tf_op jit(solution)/shard_map/concatenate | solution.py:1348
  2.7 122.1 %shard_map.203 = (bf16[4,128,1024]{2,1,0:T(8,128)(2,1)}, bf16[4,128,1024]{2,1,0:T(8,128)(2,1)}, bf16[128,1024]{1,0:T(8,128)(2,1)}, bf16[2,2,64,512]{3,2,1,0:T(8,...) custom-call(bf16[128,1024]{1,0:T(8,128)(2,1)} %refs_0_.3, bf16[128,1024]{1,0:T(8,128)(2,1)} %refs_1_.3, ...), custom_call_target="tpu_custom_call" | custom-call | tf_op jit(solution)/shard_map/pallas_call | solution.py:1395
  124.7 4.1 %shard_map.204 = (bf16[128,1024]{1,0:T(8,128)(2,1)}, f32[128,1024]{1,0:T(8,128)}, f32[64,4384]{1,0:T(8,128)}, f32[4,2304]{1,0:T(4,128)}, f32[18,128]{1,0:T(8,128...) custom-call(bf16[128,1024]{1,0:T(8,128)(2,1)} %refs_0_.3, ...), custom_call_target="tpu_custom_call" | custom-call | tf_op jit(solution)/shard_map/pallas_call | solution.py:1414

commit v3 on v2

--- a/solution.py
+++ b/solution.py
@@ -589,7 +589,7 @@
 
 LANES = 128
 FAR = -1e30
-SENDS = 130
+SENDS = 170
 exact = lax.Precision.HIGHEST
 
 
@@ -660,7 +660,9 @@
 def fused_kernel(top, *refs):
     (
         tokens, cotangent, documents, in_weight, taps, params, pre_gain, norm_gain, out_weight,
-        got_b, got_i, own_out, own_gate, own_conv, flat_all,
+        got_b, got_i, own_out, own_gate, own_conv, own_sh, flat_all,
+        sh_all, gr_sh, sib, line_sh, low_sh, high_sh, y_sh, fin_sh,
+        r_sh, r_sib, rl_sh, rh_sh, ry_sh, ro_sh,
         nall, call, docs, conv_pack, gate_pack, conv_all, gate_all, out_all,
         proj, act, dact, mk, bias_mask, step, ldec, sgate, cum, cum_t, cum_b, step_e, skip_e, scaled,
         scores, decay, weigh, inside, mixed, gates, bnorm, gain_own, sums, sums_all, totals,
@@ -726,14 +728,20 @@
         for n in range(tiles):
             at = span_of(tile_of(n, cc) + inner // LANES, LANES)
             conv[:, n * LANES : (n + 1) * LANES] = in_weight[:, at]
-        conv[:, quarter:active] = in_weight[:, 2 * inner : 2 * inner + states]
-        picked = dot(in_weight[:, 2 * inner + states :], selector(cc)[:heads].astype(bf16))
-        conv[:, active:] = picked.astype(bf16)
+
+    def pack_shared(shared):
+        shared[:, :states] = in_weight[:, 2 * inner : 2 * inner + states]
+        glob, loc = iota((heads, LANES), 0), iota((heads, LANES), 1)
+        head = loc % local_heads
+        wanted = 8 * (head // 2) + 4 * (loc // local_heads) + 2 * g + head % 2
+        pick = jnp.where((glob == wanted) & (loc < 2 * local_heads), 1.0, 0.0).astype(bf16)
+        shared[:, states:] = dot(in_weight[:, 2 * inner + states :], pick).astype(bf16)
 
     def pack_gate(gate, cc):
         for n in range(tiles):
             gate[:, n * LANES : (n + 1) * LANES] = in_weight[:, span_of(tile_of(n, cc), LANES)]
 
+    pack_shared(sh_all.at[me])
     pack(conv_all.at[me], None, c)
     pack(conv_pack, None, 1 - c)
     pl.semaphore_wait(barrier, len(greeted))
@@ -776,6 +784,34 @@
                 slot = slot_of(tt, 1 - m, cc, mid)
                 mail.arrive(all_ref.at[slot], receive.at[slot], here)
 
+    def send_shared(slot, over_y):
+        block, sem = (lambda: sh_all.at[slot]), (lambda: r_sh.at[slot])
+        if over_y:
+            mail.start(block, block, sem, dev(t, 1 - m, c))
+        mail.start(block, block, sem, dev(t + 1, m, c), t + 1 < top)
+        mail.start(block, block, sem, dev(t - 1, m, c), t >= 1)
+        mail.start(block, block, sem, dev(t, m, 1 - c))
+
+    def relay_shared(d):
+        for up in (1, -1):
+            ok = (t >= d) if up == 1 else (t + d < top)
+            onward = ok & ((t + 1 < top) if up == 1 else (t >= 1))
+            from_t = jnp.clip(t - up * d, 0, top - 1)
+            for mm in range(mid):
+                slot = slot_of(from_t, mm, c, mid)
+                mail.run(lambda slot=slot: mail.arrive(sh_all.at[slot], r_sh.at[slot], here), ok)
+                block = lambda slot=slot: sh_all.at[slot]
+                sem = lambda slot=slot: r_sh.at[slot]
+                mail.start(block, block, sem, dev(t + up, m, c), onward)
+                mail.start(block, block, sem, dev(t, m, 1 - c), ok)
+
+    def settle_shared():
+        for tt in range(top):
+            for mm in range(mid):
+                slot = slot_of(tt, mm, 1 - c, mid)
+                mail.arrive(sh_all.at[slot], r_sh.at[slot], here)
+
+    send_shared(me, True)
     spread(lambda: conv_all.at[me], conv_pack, conv_all, r_conv)
 
     floats = tokens[...].astype(f32)
@@ -787,6 +823,10 @@
 
     pack_gate(gate_all.at[me], c)
     pack_gate(gate_pack, 1 - c)
+    other_y = slot_of(t, 1 - m, c, mid)
+    mail.arrive(sh_all.at[other_y], r_sh.at[other_y], here)
+    send_shared(other_y, False)
+    relay_shared(1)
     relay(conv_all, r_conv, 1)
     spread(lambda: gate_all.at[me], gate_pack, gate_all, r_gate)
 
@@ -841,8 +881,9 @@
         gain_own[:, n * LANES : (n + 1) * LANES] = norm_gain[:, span_of(tile_of(n, c), LANES)]
 
     for d in range(2, top):
+        relay_shared(d)
         relay(conv_all, r_conv, d)
-    settle(conv_all, r_conv)
+    settle_shared()
 
     def tall(ref):
         return ref[...].reshape(total, width)
@@ -851,22 +892,14 @@
         return ref[:, :, cols].reshape(width, cols.size)
 
     wide_cols = 256
-
-    @pl.loop(0, conv_cols // wide_cols)
-    def _(n):
-        at = span_of(n, wide_cols)
-        proj[:, at] = dot(tall(nall), weights(conv_all, at)).astype(bf16)
-
-    if conv_cols % wide_cols:
-        rest = pl.ds(conv_cols - LANES, LANES)
-        proj[:, rest] = dot(tall(nall), weights(conv_all, rest)).astype(bf16)
-
-    relay(gate_all, r_gate, 1)
-    relay_rows(1)
-
+    proj[:, quarter:] = dot(tall(nall), sh_all[...].reshape(width, conv_cols - quarter)).astype(bf16)
+    shift_in = jnp.where(iota((LANES, LANES), 0) == iota((LANES, LANES), 1) + local_heads * c, 1.0, 0.0)
+    shift_in = jnp.where(iota((LANES, LANES), 1) < local_heads, shift_in, 0.0).astype(bf16)
+    shift_out = jnp.where(iota((LANES, LANES), 1) == iota((LANES, LANES), 0) + local_heads * c, 1.0, 0.0)
+    shift_out = jnp.where(iota((LANES, LANES), 0) < local_heads, shift_out, 0.0).astype(bf16)
     chosen = sharp(params[:8], selector(c))
     rate = jnp.exp(chosen[1:2])
-    raw = proj[:, active:].astype(f32) + chosen[:1]
+    raw = dot(proj[:, active:], shift_in) + chosen[:1]
     step[...] = jnp.maximum(raw, 0.0) + jnp.log1p(jnp.exp(-jnp.abs(raw)))
     sgate[...] = jax.nn.sigmoid(raw)
     ldec[...] = step[...] * -rate
@@ -881,6 +914,23 @@
         cum_t[s] = cum[at].T
     for h in range(local_heads):
         cum_b[h] = jnp.broadcast_to(cum[:, h : h + 1], (total, LANES))
+
+    settle(conv_all, r_conv)
+
+    def tall(ref):
+        return ref[...].reshape(total, width)
+
+    def weights(ref, cols):
+        return ref[:, :, cols].reshape(width, cols.size)
+
+
+    @pl.loop(0, quarter // wide_cols)
+    def _(n):
+        at = span_of(n, wide_cols)
+        proj[:, at] = dot(tall(nall), weights(conv_all, at)).astype(bf16)
+
+    relay(gate_all, r_gate, 1)
+    relay_rows(1)
 
     def conv_tile(n):
         return jnp.where(n < tiles, tile_of(n, c), n - tiles + inner // LANES)
@@ -1052,6 +1102,9 @@
     )
     conv_step = reducer(
         lambda r: gr_conv.at[r, m], y_conv, ry_conv, line_conv, low_conv, rl_conv, high_conv, rh_conv
+    )
+    sh_step = reducer(
+        lambda r: gr_sh.at[r, c], sib, r_sib, line_sh, low_sh, rl_sh, high_sh, rh_sh
     )
     order = (last, near, far, t)
     block = width // top
@@ -1124,7 +1177,7 @@
         [sharp(upper, back_cum[s * length : (s + 1) * length]) for s in range(seqs)], axis=0
     )
     back_raw = (back_step - back_decay * rate) * sgate[...]
-    bproj[:, active:] = back_raw.astype(bf16)
+    bproj[:, active:] = dot(back_raw.astype(bf16), shift_out).astype(bf16)
     flat[conv_tiles] = jnp.concatenate(
         [norm_part[:1, n * LANES : (n + 1) * LANES] for n in range(tiles)]
         + [
@@ -1156,21 +1209,14 @@
             bproj[at, cols] = dx.astype(bf16)
         flat[n] = jnp.concatenate(grads + [jnp.zeros((8 - CONV - 1, LANES), f32)], axis=0)
 
-    for r in range(top):
-        got = dot(tall_cols(nall, span_of(order[r], block)), bproj[...], contract_tokens).astype(bf16)
-        gr_conv[r] = got.reshape(gr_conv.shape[1:])
-        mail.start(
-            lambda r=r: gr_conv.at[r, 1 - m], lambda r=r: y_conv.at[r], lambda r=r: ry_conv.at[r],
-            dev(t, 1 - m, c),
-        )
-
-    gate_step(2)
-    out_step(0)
     @pl.loop(0, width // wide_cols)
     def _(n):
         at = span_of(n, wide_cols)
         slots = pl.ds(n * (wide_cols // rows), wide_cols // rows)
-        value = dot(bproj[...], conv_all[slots].reshape(wide_cols, conv_cols), contract_rows)
+        value = dot(bproj[:, :quarter], conv_all[slots].reshape(wide_cols, quarter), contract_rows)
+        value = value + dot(
+            bproj[:, quarter:], sh_all[slots].reshape(wide_cols, conv_cols - quarter), contract_rows
+        )
         value = value + dot(bgates[...], gate_all[slots].reshape(wide_cols, quarter), contract_rows)
         part_i[:, :, at] = value.astype(bf16).reshape(4, count, wide_cols)
         seen = tall_cols(nall, at).astype(f32)
@@ -1188,25 +1234,29 @@
     )
     mail.start(lambda: flat, lambda: flat_y, lambda: r_flat.at[0, 0], dev(t, 1 - m, c))
 
+    for r in range(top):
+        got = dot(tall_cols(nall, span_of(order[r], block)), bproj[...], contract_tokens).astype(bf16)
+        gr_conv[r] = got[:, :quarter].reshape(gr_conv.shape[1:])
+        for k in range(4):
+            gr_sh[r, k % 2, k // 2] = got[k * rows : (k + 1) * rows, quarter:]
+        mail.start(
+            lambda r=r: gr_sh.at[r, 1 - c], lambda r=r: sib.at[r], lambda r=r: r_sib.at[r],
+            dev(t, m, 1 - c),
+        )
+        mail.start(
+            lambda r=r: gr_conv.at[r, 1 - m], lambda r=r: y_conv.at[r], lambda r=r: ry_conv.at[r],
+            dev(t, 1 - m, c),
+        )
+
+    gate_step(2)
+    out_step(0)
     gate_step(3)
     hand_over(line_gate, own_gate, ro_gate, 0)
+    sh_step(0)
+    sh_step(1)
     out_step(1)
     out_step(2)
-    conv_step(0)
-    conv_step(1)
-    out_step(3)
-    mail.local(lambda: line_out.at[3], lambda: own_out, r_local.at[2], keeper & holder)
-    mail.start(
-        lambda: line_out.at[3], lambda: own_out, lambda: ro_out.at[0], dev_g(g, t, m, 1 - c),
-        keeper & (c != g),
-    )
-    mail.start(
-        lambda: line_out.at[3], lambda: own_out, lambda: ro_out.at[0], dev_g(1 - g, t, m, g), keeper
-    )
-    conv_step(2)
-    conv_step(3)
-    hand_over(line_conv, own_conv, ro_conv, 1)
-
+    sh_step(2)
     mail.arrive(flat_y, r_flat.at[0, 0], here)
     flat_z[t] = flat[...] + flat_y[...]
     for d in range(1, top):
@@ -1215,6 +1265,19 @@
             dev(lax.rem(t + d, top), m, c),
         )
 
+    conv_step(0)
+    conv_step(1)
+    sh_step(3)
+    mail.start(lambda: line_sh.at[3, 1 - m], lambda: y_sh, lambda: ry_sh.at[0], dev(t, 1 - m, c))
+    out_step(3)
+    mail.local(lambda: line_out.at[3], lambda: own_out, r_local.at[2], keeper & holder)
+    mail.start(
+        lambda: line_out.at[3], lambda: own_out, lambda: ro_out.at[0], dev_g(g, t, m, 1 - c),
+        keeper & (c != g),
+    )
+    mail.start(
+        lambda: line_out.at[3], lambda: own_out, lambda: ro_out.at[0], dev_g(1 - g, t, m, g), keeper
+    )
     for d in range(1, top):
         slot = lax.rem(t - d + top, top)
         mail.arrive(flat_z.at[slot], r_flat.at[1, slot], here)
@@ -1225,6 +1288,14 @@
     for slot, device in group:
         mail.start(lambda: flat_own, lambda: flat_all.at[mine], lambda: r_flat.at[2, mine], device)
     mail.local(lambda: flat_own, lambda: flat_all.at[mine], r_local.at[5])
+    conv_step(2)
+    mail.arrive(y_sh, ry_sh.at[0], here)
+    fin_sh[...] = add(line_sh[3, m], y_sh[...])
+    mail.start(lambda: fin_sh, lambda: own_sh.at[g], lambda: ro_sh.at[0], dev_g(1 - g, t, m, c))
+    mail.local(lambda: fin_sh, lambda: own_sh.at[g], r_local.at[6])
+    conv_step(3)
+    hand_over(line_conv, own_conv, ro_conv, 1)
+
     for k in range(2):
         for slot, _ in group:
             mail.arrive((got_b, got_i)[k].at[slot], r_part.at[k, slot], here)
@@ -1232,13 +1303,14 @@
     take_over(own_gate, ro_gate)
     for slot, _ in group:
         mail.arrive(flat_all.at[slot], r_flat.at[2, slot], here)
+    mail.arrive(own_sh.at[1 - g], ro_sh.at[0], here)
     take_over(own_conv, ro_conv)
     mail.finish()
 
 
 def finish_kernel(inner, heads, *refs):
     (
-        tokens, cotangent, pre_gain, got_b, got_i, own_out, own_gate, own_conv, flat_all,
+        tokens, cotangent, pre_gain, got_b, got_i, own_out, own_gate, own_conv, own_sh, flat_all,
         *targets,
     ) = refs
     outs, scratch, sems = targets[:11], targets[11:22], targets[22]
@@ -1276,9 +1348,16 @@
 
     put_tiles(0, own_gate)
     put_tiles(inner // LANES, own_conv)
-    shared = sum(own_conv[gg, cc, :, quarter:active].astype(f32) for gg, cc, _ in parts)
-    in_grad[:, 2 * inner : 2 * inner + states] = shared
-    ends = sum(dot(own_conv[gg, cc, :, active:], selector_of(gg, cc).astype(bf16)) for gg, cc, _ in parts)
+    shared = own_sh[0].astype(f32) + own_sh[1].astype(f32)
+    in_grad[:, 2 * inner : 2 * inner + states] = shared[:, :states]
+
+    def both_of(gg):
+        loc, glob = iota((LANES, LANES), 0), iota((LANES, LANES), 1)
+        head = loc % local_heads
+        wanted = 8 * (head // 2) + 4 * (loc // local_heads) + 2 * gg + head % 2
+        return jnp.where((glob == wanted) & (loc < 2 * local_heads), 1.0, 0.0).astype(bf16)
+
+    ends = sum(dot(own_sh[gg, :, states:], both_of(gg)) for gg in range(2))
     in_grad[:, 2 * inner + states :] = ends[:, :heads]
     send(2)
     out_grad[...] = own_out[...].astype(f32)
@@ -1355,17 +1434,23 @@
     V = pltpu.VMEM
     dma = pltpu.SemaphoreType.DMA
     shape = jax.ShapeDtypeStruct
+    sh_cols = conv_cols - quarter
     flat_shape = (conv_tiles + 2, 8, LANES)
     outs = [
         shape((4, count, width), bf16), shape((4, count, width), bf16), shape((own_rows, width), bf16),
-        shape((2, 2, rows, quarter), bf16), shape((2, 2, rows, conv_cols), bf16),
+        shape((2, 2, rows, quarter), bf16), shape((2, 2, rows, quarter), bf16),
+        shape((2, rows, sh_cols), bf16),
         shape((4,) + flat_shape, f32),
     ]
-    line_shapes = [(own_rows, width), (2, rows, quarter), (2, rows, conv_cols)]
+    line_shapes = [(own_rows, width), (2, rows, quarter), (2, rows, quarter)]
+    sh = (2, rows, sh_cols)
     scratch = [
+        V((shards, rows, sh_cols), bf16), V((top, 2) + sh, bf16), V((top,) + sh, bf16), V((top,) + sh, bf16),
+        V((2,) + sh, bf16), V((1,) + sh, bf16), V(sh[1:], bf16), V(sh[1:], bf16),
+        dma((shards,)), dma((top,)), dma((2,)), dma((1,)), dma((1,)), dma((1,)),
         V((4, count, width), bf16), V((4, count, width), bf16), V((2, 8, length), f32),
-        V((rows, conv_cols), bf16), V((rows, quarter), bf16),
-        V((shards, rows, conv_cols), bf16), V((shards, rows, quarter), bf16), V((top, own_rows, width), bf16),
+        V((rows, quarter), bf16), V((rows, quarter), bf16),
+        V((shards, rows, quarter), bf16), V((shards, rows, quarter), bf16), V((top, own_rows, width), bf16),
         V((total, conv_cols), bf16), V((total, active), f32), V((total, active), f32),
         V((2, CONV - 1, length, LANES), f32), V((2, length, length), f32),
         V((total, LANES), f32), V((total, LANES), f32), V((total, LANES), f32),
@@ -1380,7 +1465,7 @@
         V((2, length, length), f32), V((total, quarter), f32), V((total, quarter), f32),
         V((total, active), f32), V((8, quarter), f32), V((total, conv_cols), bf16), V((8, width), f32),
         V((top, own_rows, width), bf16), V((top, 2, 2, rows, quarter), bf16),
-        V((top, 2, 2, rows, conv_cols), bf16),
+        V((top, 2, 2, rows, quarter), bf16),
     ]
     for _ in range(4):
         scratch += [V((top,) + item, bf16) for item in line_shapes]
@@ -1390,7 +1475,7 @@
         dma((2, 4)),
     ]
     scratch += [dma((top,)) for _ in range(9)]
-    scratch += [dma((1,)), dma((2, 2)), dma((2, 2)), dma((3, max(4, top))), dma((6,))]
+    scratch += [dma((1,)), dma((2, 2)), dma((2, 2)), dma((3, max(4, top))), dma((7,))]
     hbm = pl.BlockSpec(memory_space=pl.ANY)
     results = pl.pallas_call(
         functools.partial(fused_kernel, top),
@@ -1414,7 +1499,7 @@
     final = pl.pallas_call(
         functools.partial(finish_kernel, inner, heads),
         out_shape=outs,
-        in_specs=[vmem] * 9,
+        in_specs=[vmem] * 10,
         out_specs=[hbm] * len(outs),
         scratch_shapes=[V(out.shape, out.dtype) for out in outs] + [dma((len(outs),))],
         compiler_params=pltpu.CompilerParams(vmem_limit_bytes=VMEM_LIMIT),

time: 129 us -> 122 us (0.946)
  Pallas kernels: 126 us -> 119 us
    pallas_call x1, Pallas kernels: 122 us -> 115 us  [fused(): pl.pallas_call(functools.partial(fused_kernel, top), out_shape=outs, in_s...]
where the time goes in v3:
time: 122 us
  Pallas kernels  119 us (98%)
  other arithmetic  2.02 us (2%)
    pallas_call x1, Pallas kernels, fused(): pl.pallas_call(functools.partial(fused_kernel, top), out_shape=outs, in_s...  115 us
    pallas_call x1, Pallas kernels, fused(): pl.pallas_call(functools.partial(finish_kernel, inner, heads), out_shape=...  4.06 us

profile of v3, /device:TPU:1, one launch (start us, length us, event | category | flops | bytes accessed | tf_op | source)
XLA Modules:
  0.0 121.9 jit_solution(13949866866789966731)
XLA Ops:
  0.6 0.7 select_maximum_fusion
  1.3 1.3 %pad_maximum_fusion.refs_5_ = f32[26,128]{1,0:T(8,128)} fusion(f32[18,128]{1,0:T(8,128)} %bitcast.14, f32[8,128]{1,0:T(8,128)S(1)} %select_maximum_fusion), kind=kLoop, calls=%fused_computation | loop fusion | flops 3328 | bytes 26624 | tf_op jit(solution)/shard_map/concatenate | solution.py:1427
  2.7 115.2 %shard_map.203 = (bf16[4,128,1024]{2,1,0:T(8,128)(2,1)}, bf16[4,128,1024]{2,1,0:T(8,128)(2,1)}, bf16[128,1024]{1,0:T(8,128)(2,1)}, bf16[2,2,64,512]{3,2,1,0:T(8,...) custom-call(bf16[128,1024]{1,0:T(8,128)(2,1)} %refs_0_.3, ...), custom_call_target="tpu_custom_call" | custom-call | tf_op jit(solution)/shard_map/pallas_call | solution.py:1480
  117.8 4.1 %shard_map.204 = (bf16[128,1024]{1,0:T(8,128)(2,1)}, f32[128,1024]{1,0:T(8,128)}, f32[64,4384]{1,0:T(8,128)}, f32[4,2304]{1,0:T(4,128)}, f32[18,128]{1,0:T(8,128...) custom-call(bf16[128,1024]{1,0:T(8,128)(2,1)} %refs_0_.3, ...), custom_call_target="tpu_custom_call" | custom-call | tf_op jit(solution)/shard_map/pallas_call | solution.py:1499
